TPU v7x, 128 devices: a whole 4x4x4 slice. The times are simulated.
128 devices in a mesh: heads: 8 (over z, core), width: 4 (over y), sae: 4 (over x).
Axes of the slice: x: 4, y: 4, z: 4, core: 2. Of those that a mesh axis runs over, the one named last changes fastest.
Arguments:
- x_in: bfloat16 [512, 4608], P(None, 'width'), may hold values from -64 to 64
- doc_lengths: int32 [4], replicated, may hold values from 1 to 256, 512 in all
- attn_gain: float32 [4608], P('width'), may hold values from 0.25 to 1.75
- w_query: bfloat16 [4608, 4096], P('width', 'heads'), may hold values from -0.09375 to 0.09375
- w_key: bfloat16 [4608, 2048], P('width', 'heads'), may hold values from -0.09375 to 0.09375
- w_value: bfloat16 [4608, 2048], P('width', 'heads'), may hold values from -0.09375 to 0.09375
- w_out: bfloat16 [4096, 4608], P('heads', 'width'), may hold values from -0.09375 to 0.09375
- post_gain: float32 [4608], replicated, may hold values from 0.25 to 1.75
- enc_weight: bfloat16 [4608, 65536], P(None, ('heads', 'width', 'sae')), may hold values from -0.09375 to 0.09375
- enc_bias: float32 [65536], P(('heads', 'width', 'sae')), may hold values from -1.5 to 0.5
- dec_weight: bfloat16 [65536, 4608], P(('heads', 'width', 'sae')), may hold values from -1 to 1
- dec_bias: float32 [4608], replicated, may hold values from -5 to 5
Outputs:
- grad_enc: bfloat16 [4608, 65536], P(None, ('heads', 'width', 'sae'))
- grad_dec: bfloat16 [65536, 4608], P(('heads', 'width', 'sae'))
- total_loss: float32 [], replicated
Inputs may be any that keep to these rules, and one draw needn't show every extreme that they name: `doc_lengths`: lengths of the 4 documents packed in order; they sum to 512.
All inputs are finite; a program needn't handle non-finite values.
Results may differ from a plain program's by a relative error of at most 0.02.
Values may be sent and summed in bfloat16 or wider, within the bound.
A program may use at most 128 MiB of HBM per device.

v0:
```python
import jax
import jax.numpy as jnp
from jax import lax
from jax.sharding import PartitionSpec as P

D = 4608
HEADS = 32
HEAD_DIM = 128


norm_eps = 1e-06
soft_cap = 50.0
rope_base = 10000.0
l1_weight = 3.0


def rotary(values, position):
    half_dim = values.shape[-1] // 2
    frequency = rope_base ** (-2.0 * jnp.arange(half_dim, dtype=jnp.float32) / values.shape[-1])
    angles = position.astype(jnp.float32)[:, None] * frequency[None, :]
    cosine_table = jnp.cos(angles)[:, None, :]
    sine_table = jnp.sin(angles)[:, None, :]
    first_half = values[..., :half_dim]
    second_half = values[..., half_dim:]
    return jnp.concatenate(
        [
            first_half * cosine_table - second_half * sine_table,
            second_half * cosine_table + first_half * sine_table,
        ],
        axis=-1,
    )


def attend_rows(query_rows, key_rows, value_rows, allowed_rows, scale):
    scores = (
        jnp.einsum("tkgd,skd->kgts", query_rows, key_rows, preferred_element_type=jnp.float32)
        * scale
    )
    capped = soft_cap * jnp.tanh(scores / soft_cap)
    weights = jnp.where(allowed_rows[None, None], jnp.exp(capped), 0.0)
    totals = jnp.sum(weights, axis=-1, keepdims=True)
    probs_bf = (weights / totals).astype(jnp.bfloat16)
    return jnp.einsum(
        "kgts,skd->tkgd", probs_bf, value_rows, preferred_element_type=jnp.float32
    ).astype(jnp.bfloat16)


def per_device(
    x_in,
    doc_lengths,
    attn_gain,
    w_query,
    w_key,
    w_value,
    w_out,
    post_gain,
    enc_weight,
    enc_bias,
    dec_weight,
    dec_bias,
):
    tokens = x_in.shape[0]
    query_heads = w_query.shape[1] // HEAD_DIM
    value_heads = w_key.shape[1] // HEAD_DIM
    boundary = jnp.cumsum(doc_lengths)
    position = jnp.arange(tokens, dtype=jnp.int32)
    segment = jnp.sum((boundary[None, :] <= position[:, None]).astype(jnp.int32), axis=1)
    allowed = (segment[:, None] == segment[None, :]) & (position[None, :] <= position[:, None])
    x_float = x_in.astype(jnp.float32)
    scaled = (x_float * attn_gain).astype(jnp.bfloat16)
    query_part = jnp.dot(scaled, w_query, preferred_element_type=jnp.float32)
    key_part = jnp.dot(scaled, w_key, preferred_element_type=jnp.float32)
    value_part = jnp.dot(scaled, w_value, preferred_element_type=jnp.float32)
    square_part = jnp.sum(x_float * x_float, axis=1)
    query_raw, key_raw, value_raw, square_sums = lax.psum(
        (query_part, key_part, value_part, square_part), "width"
    )
    inverse_rms = lax.rsqrt(square_sums / D + norm_eps)
    query = rotary(
        (query_raw * inverse_rms[:, None]).reshape(tokens, query_heads, HEAD_DIM), position
    ).astype(jnp.bfloat16)
    key_rows = rotary(
        (key_raw * inverse_rms[:, None]).reshape(tokens, value_heads, HEAD_DIM), position
    ).astype(jnp.bfloat16)
    value_rows = (
        (value_raw * inverse_rms[:, None])
        .reshape(tokens, value_heads, HEAD_DIM)
        .astype(jnp.bfloat16)
    )
    query4 = query.reshape(tokens, value_heads, query_heads // value_heads, HEAD_DIM)
    pieces_out = attend_rows(query4, key_rows, value_rows, allowed, (D // HEADS) ** (-0.5))
    mixed = pieces_out.reshape(tokens, query_heads * HEAD_DIM)
    proj_part = jnp.dot(mixed, w_out, preferred_element_type=jnp.float32)
    attn_sum = lax.psum(proj_part, "heads")
    attn_local = attn_sum.astype(jnp.bfloat16)
    attn_proj, x_full = (
        lax.all_gather(attn_local, "width", axis=1, tiled=True),
        lax.all_gather(x_in, "width", axis=1, tiled=True),
    )
    proj_float = attn_proj.astype(jnp.float32)
    inverse_post = lax.rsqrt(jnp.sum(proj_float * proj_float, axis=1) / D + norm_eps)
    resid = (x_full.astype(jnp.float32) + proj_float * inverse_post[:, None] * post_gain).astype(
        jnp.bfloat16
    )
    centered = (resid.astype(jnp.float32) - dec_bias).astype(jnp.bfloat16)
    pre_acts = jnp.dot(centered, enc_weight, preferred_element_type=jnp.float32) + enc_bias
    latent_acts = jnp.maximum(pre_acts, 0.0).astype(jnp.bfloat16)
    row_norms = jnp.sqrt(jnp.sum(jnp.square(dec_weight.astype(jnp.float32)), axis=1) + norm_eps)
    act_sums = jnp.sum(latent_acts.astype(jnp.float32), axis=0)
    penalty_part = jnp.sum(act_sums * row_norms)
    recon_part = jnp.dot(latent_acts, dec_weight, preferred_element_type=jnp.float32)
    recon = lax.psum(recon_part, ("heads", "width", "sae")) + dec_bias
    error = recon - resid.astype(jnp.float32)
    squares_total = jnp.sum(error * error)
    penalty_total = lax.psum(penalty_part, ("heads", "width", "sae"))
    grad_recon = (2.0 / tokens * error).astype(jnp.bfloat16)
    total_loss = (squares_total + l1_weight * penalty_total) / (tokens * D)
    upstream = lax.dot_general(
        grad_recon, dec_weight, (((1,), (1,)), ((), ())), preferred_element_type=jnp.float32
    )
    grad_pre = jnp.where(pre_acts > 0, upstream + l1_weight * row_norms / tokens, 0.0).astype(
        jnp.bfloat16
    )
    grad_enc = lax.dot_general(
        centered, grad_pre, (((0,), (0,)), ((), ())), preferred_element_type=jnp.float32
    ).astype(jnp.bfloat16)
    decoder_term = lax.dot_general(
        latent_acts, grad_recon, (((0,), (0,)), ((), ())), preferred_element_type=jnp.float32
    )
    grad_dec = (
        decoder_term
        + l1_weight
        / tokens
        * act_sums[:, None]
        * dec_weight.astype(jnp.float32)
        / row_norms[:, None]
    ).astype(jnp.bfloat16)
    return (grad_enc, grad_dec, total_loss)


def solution(mesh):
    placed = (
        P(None, "width"),
        P(),
        P("width"),
        P("width", "heads"),
        P("width", "heads"),
        P("width", "heads"),
        P("heads", "width"),
        P(),
        P(None, ("heads", "width", "sae")),
        P(("heads", "width", "sae")),
        P(("heads", "width", "sae"), None),
        P(),
    )
    return jax.shard_map(
        per_device,
        mesh=mesh,
        in_specs=placed,
        out_specs=(P(None, ("heads", "width", "sae")), P(("heads", "width", "sae"), None), P()),
        check_vma=False,
    )
```

profile of v0, /device:TPU:1, one launch (start us, length us, event | category | flops | bytes accessed | tf_op | source)
XLA Modules:
  0.0 471.6 jit_solution(9375944868353371698)
XLA Ops:
  7.3 3.6 fusion.23
  10.9 2.7 fusion.25
  13.6 1.3 fusion.27
  15.5 9.5 %psum.50 = f32[512]{0:T(512)S(1)} all-reduce(f32[512]{0:T(512)S(1)} %fusion.14), channel_id=1, replica_groups=mesh['heads'=8,'width'=4,'sae'=4] {'width'}, use_global_device_ids=true, to_apply=%region_2.3 | all-reduce | flops 512 | bytes 4096 | tf_op jit(solution)/shard_map/psum | solution.py:75
  25.2 0.9 fusion.22
  26.1 1.7 multiply_cosine_fusion
  27.8 49.0 %all-reduce.7.cloned.1.call-done = (f32[512,256]{1,0:T(8,128)}, f32[512,512]{1,0:T(8,128)}, f32[512,256]{1,0:T(8,128)}) async-done(((f32[512,256]{1,0:T(8,128)}, f32[512,512]{1,0:T(8,128)}, f32[512,256]{1,0:T(8,128)}), (f32[512,256]{1,0:T(8,128)}, f32[512,512]{1,0:T(8,128)}, f32[512,256]{1,0:T(8,128)})) %all-reduce.7.cloned.1.call-update) | async-done | bytes 2097168 | tf_op jit(solution)/shard_map/psum | solution.py:75
  76.9 2.1 broadcast_multiply_fusion.1
  79.2 1.5 fusion.40
  80.7 1.4 broadcast_multiply_fusion
  82.1 0.4 reshape.169
  82.5 1.8 subtract_convert_fusion
  84.6 1.3 subtract_convert_fusion.1
  85.9 2.9 fusion.12
  88.8 1.6 fusion.21
  90.4 0.9 fusion.41
  91.3 52.5 %all-reduce.8 = bf16[512,1152]{1,0:T(8,128)(2,1)} all-reduce(f32[512,1152]{1,0:T(8,128)S(1)} %fusion.41), channel_id=1, replica_groups=mesh['heads'=8,'width'=4,'sae'=4] {'heads'}, use_global_device_ids=true, to_apply=%region_8.9 | all-reduce | flops 589824 | bytes 3538944 | tf_op jit(solution)/shard_map/psum | solution.py:94
  143.8 0.7 all-gather.3.cloned.1.call-update
  144.8 51.8 %all-gather.5.cloned.1.call-done = bf16[512,4608]{1,0:T(8,128)(2,1)} async-done(((bf16[512,1152]{1,0:T(8,128)(2,1)}), bf16[512,4608]{1,0:T(8,128)(2,1)}) %all-gather.5.cloned.1.call-update) | async-done | bytes 4718608 | tf_op jit(solution)/shard_map/all_gather | solution.py:97
  196.6 3.3 fusion
  200.0 51.3 %all-gather.3.cloned.1.call-done = bf16[512,4608]{1,0:T(8,128)(2,1)} async-done(((bf16[512,1152]{1,0:T(8,128)(2,1)}), bf16[512,4608]{1,0:T(8,128)(2,1)}) %all-gather.3.cloned.1.call-update) | async-done | bytes 4718608 | tf_op jit(solution)/shard_map/all_gather | solution.py:98
  251.3 5.9 %fusion.3 = bf16[512,4608]{1,0:T(8,128)(2,1)S(1)} fusion(bf16[512,4608]{1,0:T(8,128)(2,1)} %all-gather.5.cloned.1.call-done, bf16[512,4608]{1,0:T(8,128)(2,1)} %all-gather.3.cloned.1.call-done, f32[4608]{0:T(1024)S(1)} %copy-done.8, f32[512]{0:T(512)S(1)} %add_rsqrt_fusion), kind=kLoop, calls=%fused_computation.9 | loop fusion | flops 14155776 | bytes 14176256 | tf_op jit(solution)/shard_map/convert_element_type | solution.py:102
  257.3 6.4 %convert_reduce_fusion = (f32[512]{0:T(512)S(1)}, f32[512,512]{1,0:T(8,128)S(1)}) fusion(f32[512]{0:T(512)S(1)} %copy-done.12, bf16[4608,512]{1,0:T(8,128)(2,1)} %param.20, bf16[512,4608]{1,0:T(8,128)(2,1)S(1)} %fusion.3, f32[4608]{0:T(1024)S(1)} %copy-done.9), kind=kOutput, calls=%fused_computation.32 | convolution fusion | flops 2424045056 | bytes 10508288 | tf_op jit(solution)/shard_map/dot_general | solution.py:106
  263.7 5.1 %fusion.39 = f32[512,4608]{1,0:T(8,128)} fusion(bf16[512,4608]{1,0:T(8,128)(2,1)S(1)} %bitcast.41, f32[512,512]{1,0:T(8,128)S(1)} %get-tuple-element.25), kind=kOutput, calls=%fused_computation.69 | convolution fusion | flops 2416443392 | bytes 15204352 | tf_op jit(solution)/shard_map/dot_general | solution.py:111
  268.8 3.3 fusion.5
  272.2 0.6 multiply_reduce_fusion.1
  272.8 65.8 %psum.55 = f32[]{:T(128)} all-reduce(f32[]{:T(128)} %get-tuple-element.16), channel_id=1, replica_groups=mesh['heads'=8,'width'=4,'sae'=4] {'heads','width','sae'}, use_global_device_ids=true, to_apply=%region_15.16 | all-reduce | flops 1 | bytes 8 | tf_op jit(solution)/shard_map/psum | solution.py:115
  339.2 94.4 %all-reduce.5.cloned.1.call-done = f32[512,4608]{1,0:T(8,128)} async-done(((f32[512,4608]{1,0:T(8,128)}), f32[512,4608]{1,0:T(8,128)}) %all-reduce.5.cloned.1.call-update) | async-done | bytes 9437200 | tf_op jit(solution)/shard_map/psum | solution.py:112
  433.6 8.4 %multiply_reduce_fusion = (f32[]{:T(128)}, bf16[512,4608]{1,0:T(8,128)(2,1)S(1)}) fusion(bf16[512,4608]{1,0:T(8,128)(2,1)} %copy-done.2, f32[512,4608]{1,0:T(8,128)} %all-reduce.5.cloned.1.call-done, f32[4608]{0:T(1024)S(1)} %copy-done.9), kind=kLoop, calls=%fused_computation.15 | loop fusion | flops 16515071 | bytes 18892804 | tf_op jit(solution)/shard_map/reduce_sum | solution.py:114
  442.0 6.7 %fusion.20 = bf16[512,512]{1,0:T(8,128)(2,1)S(1)} fusion(bf16[512,4608]{1,0:T(8,128)(2,1)S(1)} %get-tuple-element.7, bf16[512,4608]{1,0:T(8,128)(2,1)} %param.22, f32[512,512]{1,0:T(8,128)S(1)} %get-tuple-element.25, f32[512]{0:T(512)S(1)} %get-tuple-element.17), kind=kOutput, calls=%fused_computation.30 | convolution fusion | flops 2416967680 | bytes 11012096 | tf_op jit(solution)/shard_map/dot_general | solution.py:118
  448.7 6.8 %convolution_convert_fusion = bf16[4608,512]{1,0:T(8,128)(2,1)} fusion(bf16[512,512]{1,0:T(8,128)(2,1)S(1)} %fusion.20, bf16[512,4608]{1,0:T(8,128)(2,1)} %copy-done.2, f32[4608]{0:T(1024)S(1)} %copy-done.9), kind=kOutput, calls=%fused_computation.17 | convolution fusion | flops 2425356288 | bytes 9979904 | tf_op jit(solution)/shard_map/dot_general | solution.py:124
  456.1 7.8 %fusion.8 = bf16[512,4608]{1,0:T(8,128)(2,1)} fusion(bf16[512,4608]{1,0:T(8,128)(2,1)} %param.22, bf16[512,4608]{1,0:T(8,128)(2,1)} %copy-done.4, f32[512]{0:T(512)S(1)} %get-tuple-element.18, f32[512]{0:T(512)S(1)} %get-tuple-element.19, f32[512,512]{1,0:T(8,128)S(1)} %get-tuple-element.25), kind=kOutput, calls=%fused_computation.14 | convolution fusion | flops 2428239872 | bytes 15208448 | tf_op jit(solution)/shard_map/dot_general | solution.py:127
  (51 shorter events, 1.6 us)
Async XLA Ops:
  7.2 83.3 %copy-start = (bf16[512,1152]{1,0:T(8,128)(2,1)S(1)}, bf16[512,1152]{1,0:T(8,128)(2,1)}, u32[]{:S(2)}) copy-start(bf16[512,1152]{1,0:T(8,128)(2,1)} %param.18) | copy-start | bytes 3538948
  7.2 6.5 %copy-start.3 = (bf16[512,1152]{1,0:T(8,128)(2,1)S(1)}, bf16[512,1152]{1,0:T(8,128)(2,1)}, u32[]{:S(2)}) copy-start(bf16[512,1152]{1,0:T(8,128)(2,1)} %param.12) | copy-start | bytes 3538948
  7.2 6.4 %copy-start.11 = (f32[1152]{0:T(1024)S(1)}, f32[1152]{0:T(1024)}, u32[]{:S(2)}) copy-start(f32[1152]{0:T(1024)} %param.14) | copy-start | bytes 13828
  7.2 6.4 %copy-start.10 = (bf16[1152,256]{1,0:T(8,128)(2,1)S(1)}, bf16[1152,256]{1,0:T(8,128)(2,1)}, u32[]{:S(2)}) copy-start(bf16[1152,256]{1,0:T(8,128)(2,1)} %param.17) | copy-start | bytes 1769476
  7.2 7.8 %copy-start.13 = (s32[4]{0:T(128)S(1)}, s32[4]{0:T(128)}, u32[]{:S(2)}) copy-start(s32[4]{0:T(128)} %param.13) | copy-start | bytes 52
  7.2 69.6 %all-reduce.7.cloned.1.call-start = ((), (), s32[]{:S(2)}) async-start(), calls=%async_computation.3 | async-start | bytes 4194304 | tf_op jit(solution)/shard_map/psum | solution.py:75
  15.0 181.6 %all-gather.5.cloned.1.call-start = ((), (), s32[]{:S(2)}) async-start(), calls=%async_computation.1 | async-start | bytes 5898240 | tf_op jit(solution)/shard_map/all_gather | solution.py:97
  82.4 2.0 copy-start.6
  82.4 2.1 copy-start.5
  85.9 2.9 copy-start.7
  91.3 160.0 %copy-start.8 = (f32[4608]{0:T(1024)S(1)}, f32[4608]{0:T(1024)}, u32[]{:S(2)}) copy-start(f32[4608]{0:T(1024)} %param.19) | copy-start | bytes 55300
  143.8 107.5 %all-gather.3.cloned.1.call-start = ((), (), s32[]{:S(2)}) async-start(), calls=%async_computation | async-start | bytes 5898240 | tf_op jit(solution)/shard_map/all_gather | solution.py:98
  144.5 289.1 %all-reduce.5.cloned.1.call-start = ((), (), s32[]{:S(2)}) async-start(), calls=%async_computation.2 | async-start | bytes 18874368 | tf_op jit(solution)/shard_map/psum | solution.py:112
  199.9 57.3 %copy-start.9 = (f32[4608]{0:T(1024)S(1)}, f32[4608]{0:T(1024)}, u32[]{:S(2)}) copy-start(f32[4608]{0:T(1024)} %param.23) | copy-start | bytes 55300
  199.9 57.3 %copy-start.12 = (f32[512]{0:T(512)S(1)}, f32[512]{0:T(512)}, u32[]{:S(2)}) copy-start(f32[512]{0:T(512)} %param.21) | copy-start | bytes 6148
  251.3 12.4 %slice-start = ((s8[4718592]{0:T(1024)(128)(4,1)}), s8[4194304]{0:T(1024)(128)(4,1)S(1)}, s32[]{:S(2)}) async-start(s8[4718592]{0:T(1024)(128)(4,1)} %bitcast.40), calls=%async_computation.4 | async-start | bytes 8388608
  257.2 6.4 %copy-start.2 = (bf16[512,4608]{1,0:T(8,128)(2,1)}, bf16[512,4608]{1,0:T(8,128)(2,1)S(1)}, u32[]{:S(2)}) copy-start(bf16[512,4608]{1,0:T(8,128)(2,1)S(1)} %fusion.3) | copy-start | bytes 14155780
  257.2 6.5 %slice-start.1 = ((s8[4718592]{0:T(1024)(128)(4,1)}), s8[524288]{0:T(1024)(128)(4,1)S(1)}, s32[]{:S(2)}) async-start(s8[4718592]{0:T(1024)(128)(4,1)} %bitcast.40), calls=%async_computation.5 | async-start | bytes 1048576
  442.0 6.7 %copy-start.4 = (bf16[512,4608]{1,0:T(8,128)(2,1)}, bf16[512,4608]{1,0:T(8,128)(2,1)S(1)}, u32[]{:S(2)}) copy-start(bf16[512,4608]{1,0:T(8,128)(2,1)S(1)} %get-tuple-element.7) | copy-start | bytes 14155780
  456.1 7.9 %copy-start.1 = (bf16[512,1152]{1,0:T(8,128)(2,1)S(1)}, bf16[512,1152]{1,0:T(8,128)(2,1)}, u32[]{:S(2)}) copy-start(bf16[512,1152]{1,0:T(8,128)(2,1)} %param.18) | copy-start | bytes 3538948
Sparse Core Ops, SparseCore 0:
  15.1 61.7 all-reduce.6
  143.9 52.6 all-gather.4
  198.3 52.9 all-gather.2
  268.9 164.6 all-reduce.4
where the time goes:
time: 472 us
  waiting for transfers between devices  247 us (52%)
  blocking collectives  128 us (27%)
  matrix products  45.7 us (10%)
  other arithmetic  31.4 us (7%)
  between operations  16.5 us (3%)
    psum x1, waiting for transfers between devices, per_device(): recon = lax.psum(recon_part, ('heads', 'width', 'sae')) + dec_bias  94.4 us
    psum x1, blocking collectives, per_device(): penalty_total = lax.psum(penalty_part, ('heads', 'width', 'sae'))  65.8 us
    psum x1, blocking collectives, per_device(): attn_sum = lax.psum(proj_part, 'heads')  52.5 us
    all_gather x1, waiting for transfers between devices, per_device(): lax.all_gather(attn_local, 'width', axis=1, tiled=True)  51.8 us
    all_gather x1, waiting for transfers between devices, per_device(): lax.all_gather(x_in, 'width', axis=1, tiled=True)  51.3 us
    psum x1, waiting for transfers between devices, per_device(): lax.psum((query_part, key_part, value_part, square_part), 'width')  49 us
    psum x1, blocking collectives, per_device(): lax.psum((query_part, key_part, value_part, square_part), 'width')  9.54 us
  transfers between devices with their start and end apart: 4, of which 4 were waited for; matrix products, arithmetic and copies ran while one was open for 2% of the time, Pallas kernels for 0%

commit v1 on v0

v1 whole, which is shorter than its diff:
```python
import functools

import jax
import jax.numpy as jnp
import numpy as np
from jax import lax
from jax.experimental import pallas as pl
from jax.experimental.pallas import tpu as pltpu
from jax.sharding import PartitionSpec as P

D = 4608
HEADS = 32
HEAD_DIM = 128
TOKENS = 512

norm_eps = 1e-06
soft_cap = 50.0
rope_base = 10000.0
l1_weight = 3.0

MESH = pl.DeviceIdType.MESH
BF = jnp.bfloat16
F32 = jnp.float32
HIGHEST = lax.Precision.HIGHEST

ORDERS = (("y", "x", "z"), ("x", "z", "y"), ("z", "y", "x"))


class Nav:
    def __init__(self):
        self.h = lax.axis_index("heads")
        self.y = lax.axis_index("width")
        self.x = lax.axis_index("sae")
        self.z = self.h // 2
        self.c = self.h % 2

    def index(self, axis):
        return {"x": self.x, "y": self.y, "z": self.z}[axis]

    def peer(self, axis, d):
        if axis == "c":
            return {"heads": self.z * 2 + (1 - self.c)}
        if axis == "h":
            return {"heads": (self.h + d) % 8}
        if axis == "z":
            return {"heads": ((self.z + d) % 4) * 2 + self.c}
        if axis == "y":
            return {"width": (self.y + d) % 4}
        return {"sae": (self.x + d) % 4}


def send(src, dst, ssem, rsem, device):
    copy = pltpu.make_async_remote_copy(
        src_ref=src, dst_ref=dst, send_sem=ssem, recv_sem=rsem, device_id=device, device_id_type=MESH
    )
    copy.start()
    return copy


def barrier(nav):
    sem = pltpu.get_barrier_semaphore()
    peers = [("h", d) for d in range(1, 8)] + [(a, d) for a in "xy" for d in (1, 2, 3)]
    for axis, d in peers:
        pl.semaphore_signal(sem, inc=1, device_id=nav.peer(axis, d), device_id_type=MESH)
    pl.semaphore_wait(sem, len(peers))


def gather_sems():
    dma = pltpu.SemaphoreType.DMA
    return [dma((3, 3)), dma((3, 3)), dma((3, 3)), dma((3, 3)), dma((3, 4, 3)), dma((3, 4, 3)), dma((3, 4, 4)), dma((3, 4, 4))]


def all_gather(nav, full, sems):
    s1, r1, s2, r2, s3, r3, sc, rc = sems
    c = nav.c
    sent, first, second, third, core = [], {}, {}, {}, []
    place = [[nav.index(a) for a in order] for order in ORDERS]

    def share(p, k3, k2, slot3, slot2):
        part = full.at[p, c, k3, k2]
        core.append(send(part, part, sc.at[p, slot3, slot2], rc.at[p, slot3, slot2], nav.peer("c", 1)))

    for p, order in enumerate(ORDERS):
        i1, i2, i3 = place[p]
        block = full.at[p, c, i3, i2, i1]
        for d in (1, 2, 3):
            first[p, d] = send(block, block, s1.at[p, d - 1], r1.at[p, d - 1], nav.peer(order[0], d))
    for p, order in enumerate(ORDERS):
        i1, i2, i3 = place[p]
        for d in (1, 2, 3):
            first[p, d].wait_recv()
        part = full.at[p, c, i3, i2]
        for d in (1, 2, 3):
            second[p, d] = send(part, part, s2.at[p, d - 1], r2.at[p, d - 1], nav.peer(order[1], d))
        for d in (1, 2, 3):
            third[p, 0, d] = send(part, part, s3.at[p, 0, d - 1], r3.at[p, 0, d - 1], nav.peer(order[2], d))
        share(p, i3, i2, 0, 0)
    for e in (1, 3, 2):
        for p, order in enumerate(ORDERS):
            i1, i2, i3 = place[p]
            second[p, e].wait_recv()
            k2 = (i2 + 4 - e) % 4
            part = full.at[p, c, i3, k2]
            for d in (1, 2, 3):
                third[p, e, d] = send(part, part, s3.at[p, e, d - 1], r3.at[p, e, d - 1], nav.peer(order[2], d))
            share(p, i3, k2, 0, e)
    for e in (0, 1, 3, 2):
        for d in (1, 3, 2):
            for p, order in enumerate(ORDERS):
                i1, i2, i3 = place[p]
                third[p, e, d].wait_recv()
                share(p, (i3 + 4 - d) % 4, (i2 + 4 - e) % 4, d, e)
    for copy in core:
        copy.wait_recv()
    for group in (first, second, third):
        for copy in group.values():
            copy.wait_send()
    for copy in core:
        copy.wait_send()


def unpack(full, out, sem):
    for p, order in enumerate(ORDERS):
        where = {a: k for k, a in enumerate(order)}
        for c in range(2):
            for y in range(4):
                for z in range(4):
                    idx = [None, None, None]
                    idx[where["y"]] = y
                    idx[where["z"]] = z
                    idx[where["x"]] = slice(None)
                    src = full.at[p, c, idx[2], idx[1], idx[0]]
                    dst = out.at[:, z, c, :, y * 1152 + p * 384 : y * 1152 + (p + 1) * 384]
                    pltpu.make_async_copy(src, dst, sem).start()
    pltpu.make_async_copy(out, out, sem).wait()


def front_kernel(
    doc_ref, gain_ref, post_ref, bias_ref, x_hbm, cos_hbm, sin_hbm, wq_hbm, wk_hbm, wv_hbm, wo_hbm,
    resid_ref, out_hbm,
    xv, cosv, sinv, wq, wk, wv, wo, lsem,
    part32, part16, got1, ss1, got_ss, s1, r1, s1b, r1b,
    kv, s3, r3, mixed, s5, r5, proj, got7, s7, r7, sq8, got8, s8, r8,
    full, osem, *sems,
):
    nav = Nav()
    h, y, x = nav.h, nav.y, nav.x
    rows = pl.ds(pl.multiple_of(x * 128, 128), 128)
    loads = []
    for k, (src, dst) in enumerate(
        [(x_hbm.at[rows], xv), (wq_hbm, wq), (wk_hbm, wk), (wv_hbm, wv), (cos_hbm.at[rows], cosv), (sin_hbm.at[rows], sinv), (wo_hbm, wo)]
    ):
        copy = pltpu.make_async_copy(src, dst, lsem.at[k])
        copy.start()
        loads.append(copy)
    barrier(nav)
    loads[0].wait()
    xf = xv[...].astype(F32)
    ss1[...] = lax.dot_general(
        jnp.ones((8, 1152), F32), xf * xf, (((1,), (1,)), ((), ())), precision=HIGHEST, preferred_element_type=F32
    )
    square = [send(ss1, got_ss.at[d - 1], s1b.at[d - 1], r1b.at[d - 1], nav.peer("y", d)) for d in (1, 2, 3)]
    scaled = (xf * gain_ref[...]).astype(BF)
    loads[1].wait()
    loads[2].wait()
    loads[3].wait()
    for kvh in range(2):
        cols = slice(kvh * 128, kvh * 128 + 128)
        key = jnp.dot(scaled, wk[:, cols], preferred_element_type=F32)
        val = jnp.dot(scaled, wv[:, cols], preferred_element_type=F32)
        for g in range(2):
            w = kvh * 2 + g
            q = jnp.dot(scaled, wq[:, w * 128 : w * 128 + 128], preferred_element_type=F32)
            for k, t in enumerate((q, key, val)):
                part32[w, :, k * 128 : k * 128 + 128] = t
                part16[w, :, k * 128 : k * 128 + 128] = t.astype(BF)
    moved = [send(part16.at[(y + d) % 4], got1.at[d - 1], s1.at[d - 1], r1.at[d - 1], nav.peer("y", d)) for d in (1, 2, 3)]
    for copy in square:
        copy.wait_recv()
    total = ss1[...] + got_ss[0] + got_ss[1] + got_ss[2]
    spread = lax.dot_general(
        total, jnp.full((8, 128), 0.125, F32), (((0,), (0,)), ((), ())), precision=HIGHEST, preferred_element_type=F32
    )
    inverse = lax.rsqrt(spread / D + norm_eps)
    loads[4].wait()
    loads[5].wait()
    for copy in moved:
        copy.wait_recv()
    qkv = []
    for k in range(3):
        cols = slice(k * 128, k * 128 + 128)
        t = part32[y, :, cols] + got1[0, :, cols].astype(F32) + got1[1, :, cols].astype(F32) + got1[2, :, cols].astype(F32)
        t = t * inverse
        if k < 2:
            t = t * cosv[...] + pltpu.roll(t, 64, 1) * sinv[...]
        qkv.append(t.astype(BF))
    kv[x, :, 0:128] = qkv[1]
    kv[x, :, 128:256] = qkv[2]
    spreads = [send(kv.at[x], kv.at[x], s3.at[d - 1], r3.at[d - 1], nav.peer("x", d)) for d in (1, 2, 3)]
    bounds = []
    run = 0
    for j in range(4):
        run = run + doc_ref[j]
        bounds.append(run)
    qpos = x * 128 + lax.broadcasted_iota(jnp.int32, (128, 512), 0)
    kpos = lax.broadcasted_iota(jnp.int32, (128, 512), 1)
    qseg = sum((b <= qpos).astype(jnp.int32) for b in bounds)
    kseg = sum((b <= kpos).astype(jnp.int32) for b in bounds)
    allowed = (qseg == kseg) & (kpos <= qpos)
    for copy in spreads:
        copy.wait_recv()
    keys = kv[:, :, 0:128].reshape(512, 128)
    vals = kv[:, :, 128:256].reshape(512, 128)
    scores = lax.dot_general(qkv[0], keys, (((1,), (1,)), ((), ())), preferred_element_type=F32) * ((D // HEADS) ** -0.5)
    capped = soft_cap * jnp.tanh(scores / soft_cap)
    weights = jnp.where(allowed, jnp.exp(capped), 0.0)
    probs = (weights / jnp.sum(weights, axis=-1, keepdims=True)).astype(BF)
    mixed[y] = jnp.dot(probs, vals, preferred_element_type=F32).astype(BF)
    mixes = [send(mixed.at[y], mixed.at[y], s5.at[d - 1], r5.at[d - 1], nav.peer("y", d)) for d in (1, 2, 3)]
    loads[6].wait()
    for copy in mixes:
        copy.wait_recv()
    whole = jnp.concatenate([mixed[w] for w in range(4)], axis=1)
    for k in range(3):
        cols = slice(k * 384, k * 384 + 384)
        t = jnp.dot(whole, wo[:, cols], preferred_element_type=F32).astype(BF)
        proj[:, :, cols] = t.reshape(8, 16, 384)
    parts = [send(proj.at[(h + d) % 8], got7.at[d - 1], s7.at[d - 1], r7.at[d - 1], nav.peer("h", d)) for d in range(1, 8)]
    for copy in parts:
        copy.wait_recv()
    acc = proj[h].astype(F32)
    for d in range(7):
        acc = acc + got7[d].astype(F32)
    acc = acc.astype(BF).astype(F32)
    sq8[...] = jnp.broadcast_to(jnp.sum(acc * acc, axis=1, keepdims=True), (16, 128))
    norms = [send(sq8, got8.at[d - 1], s8.at[d - 1], r8.at[d - 1], nav.peer("y", d)) for d in (1, 2, 3)]
    for copy in norms:
        copy.wait_recv()
    tot8 = sq8[...] + got8[0] + got8[1] + got8[2]
    inverse_post = lax.rsqrt(tot8 / D + norm_eps)[:, 0:1]
    own_x = xv[pl.ds(pl.multiple_of(h * 16, 16), 16), :].astype(F32)
    resid = (own_x + acc * inverse_post * post_ref[y]).astype(BF)
    resid_ref[...] = resid
    centered = (resid.astype(F32) - bias_ref[y]).astype(BF)
    for p, order in enumerate(ORDERS):
        i1, i2, i3 = [nav.index(a) for a in order]
        full[p, nav.c, i3, i2, i1] = centered[:, p * 384 : p * 384 + 384]
    all_gather(nav, full, sems)
    for group in (square, moved, spreads, mixes, parts, norms):
        for copy in group:
            copy.wait_send()
    unpack(full, out_hbm, osem)


def front(doc, gain, post, bias, x_in, cos, sin, wq, wk, wv, wo):
    dma = pltpu.SemaphoreType.DMA
    vmem = pl.BlockSpec(memory_space=pltpu.VMEM)
    anyspace = pl.BlockSpec(memory_space=pl.ANY)
    return pl.pallas_call(
        front_kernel,
        name="front",
        out_shape=(jax.ShapeDtypeStruct((16, 1152), BF), jax.ShapeDtypeStruct((4, 4, 2, 16, D), BF)),
        in_specs=[pl.BlockSpec(memory_space=pltpu.SMEM)] + [vmem] * 3 + [anyspace] * 7,
        out_specs=(vmem, anyspace),
        scratch_shapes=[
            pltpu.VMEM((128, 1152), BF), pltpu.VMEM((128, 128), F32), pltpu.VMEM((128, 128), F32),
            pltpu.VMEM((1152, 512), BF), pltpu.VMEM((1152, 256), BF), pltpu.VMEM((1152, 256), BF),
            pltpu.VMEM((512, 1152), BF), dma((7,)),
            pltpu.VMEM((4, 128, 384), F32), pltpu.VMEM((4, 128, 384), BF), pltpu.VMEM((3, 128, 384), BF),
            pltpu.VMEM((8, 128), F32), pltpu.VMEM((3, 8, 128), F32), dma((3,)), dma((3,)), dma((3,)), dma((3,)),
            pltpu.VMEM((4, 128, 256), BF), dma((3,)), dma((3,)),
            pltpu.VMEM((4, 128, 128), BF), dma((3,)), dma((3,)),
            pltpu.VMEM((8, 16, 1152), BF), pltpu.VMEM((7, 16, 1152), BF), dma((7,)), dma((7,)),
            pltpu.VMEM((16, 128), F32), pltpu.VMEM((3, 16, 128), F32), dma((3,)), dma((3,)),
            pltpu.VMEM((3, 2, 4, 4, 4, 16, 384), BF), dma(()),
        ] + gather_sems(),
        compiler_params=pltpu.CompilerParams(collective_id=0, has_side_effects=True, vmem_limit_bytes=60 << 20),
    )(doc, gain, post, bias, x_in, cos, sin, wq, wk, wv, wo)


def back_kernel(
    acts_hbm, dec_hbm, resid_ref, bias_ref, pen_ref,
    out_hbm, loss_ref,
    acts, dec, lsem, part, got0, s0, r0, got3, s3, r3, slab, got2, s2, r2, strip, got1, s1, r1,
    mine, gotl, sl, rl, full, osem, *sems,
):
    nav = Nav()
    c = nav.c
    place = [[nav.index(a) for a in order] for order in ORDERS]
    load_a = pltpu.make_async_copy(acts_hbm, acts, lsem.at[0])
    load_a.start()
    load_d = pltpu.make_async_copy(dec_hbm, dec, lsem.at[1])
    load_d.start()
    barrier(nav)
    load_a.wait()
    load_d.wait()
    left = acts[...]
    for p, order in enumerate(ORDERS):
        where = {a: k for k, a in enumerate(order)}

        def chunk(w, carry, p=p, where=where):
            cols = pl.ds(pl.multiple_of(w * 1152 + p * 384, 128), 384)
            t = jnp.dot(left, dec[:, cols], preferred_element_type=F32).astype(BF)
            for xx in range(4):
                for zz in range(4):
                    for cc in range(2):
                        idx = [None, None, None]
                        idx[where["x"]] = xx
                        idx[where["z"]] = zz
                        idx[where["y"]] = w
                        r = xx * 128 + zz * 32 + cc * 16
                        part[p, cc, idx[2], idx[1], idx[0]] = t[r : r + 16]
            return carry

        lax.fori_loop(0, 4, chunk, 0)
    swap = {}
    for p in range(3):
        for d in (1, 2, 3, 0):
            t3 = (place[p][2] + d) % 4
            swap[p, d] = send(part.at[p, 1 - c, t3], got0.at[p, t3], s0.at[p, d], r0.at[p, d], nav.peer("c", 1))
    third = {}
    for d in (2, 1, 3):
        for p, order in enumerate(ORDERS):
            t3 = (place[p][2] + d) % 4
            swap[p, d].wait_recv()
            part[p, c, t3] = (part[p, c, t3].astype(F32) + got0[p, t3].astype(F32)).astype(BF)
            third[p, d] = send(part.at[p, c, t3], got3.at[p, d - 1], s3.at[p, d - 1], r3.at[p, d - 1], nav.peer(order[2], d))
    second, first = {}, {}
    for p, order in enumerate(ORDERS):
        i1, i2, i3 = place[p]
        swap[p, 0].wait_recv()
        for d in (1, 2, 3):
            third[p, d].wait_recv()
        t = part[p, c, i3].astype(F32) + got0[p, i3].astype(F32)
        for d in range(3):
            t = t + got3[p, d].astype(F32)
        slab[p] = t.astype(BF)
        for d in (2, 1, 3):
            second[p, d] = send(slab.at[p, (i2 + d) % 4], got2.at[p, d - 1], s2.at[p, d - 1], r2.at[p, d - 1], nav.peer(order[1], d))
    for p, order in enumerate(ORDERS):
        i1, i2, i3 = place[p]
        for d in (1, 2, 3):
            second[p, d].wait_recv()
        t = slab[p, i2].astype(F32)
        for d in range(3):
            t = t + got2[p, d].astype(F32)
        strip[p] = t.astype(BF)
        for d in (2, 1, 3):
            first[p, d] = send(strip.at[p, (i1 + d) % 4], got1.at[p, d - 1], s1.at[p, d - 1], r1.at[p, d - 1], nav.peer(order[0], d))
    squares = jnp.zeros((16, 384), F32)
    for p, order in enumerate(ORDERS):
        i1, i2, i3 = place[p]
        cols = slice(p * 384, p * 384 + 384)
        for d in (1, 2, 3):
            first[p, d].wait_recv()
        t = strip[p, i1].astype(F32)
        for d in range(3):
            t = t + got1[p, d].astype(F32)
        error = t + bias_ref[nav.y][:, cols] - resid_ref[:, cols].astype(F32)
        squares = squares + error * error
        full[p, c, i3, i2, i1] = (2.0 / TOKENS * error).astype(BF)
    all_gather(nav, full, sems)
    mine[0] = jnp.broadcast_to(jnp.sum(squares, keepdims=True), (8, 128)) + l1_weight * pen_ref[...]
    losses = []
    for k, (axis, n) in enumerate((("h", 8), ("y", 4), ("x", 4))):
        group = [send(mine.at[k], gotl.at[k, d - 1], sl.at[k, d - 1], rl.at[k, d - 1], nav.peer(axis, d)) for d in range(1, n)]
        total = mine[k]
        for copy in group:
            copy.wait_recv()
        for d in range(n - 1):
            total = total + gotl[k, d]
        mine[k + 1] = total
        losses += group
    loss_ref[...] = mine[3] / (TOKENS * D)
    for group in (swap, third, second, first):
        for copy in group.values():
            copy.wait_send()
    for copy in losses:
        copy.wait_send()
    unpack(full, out_hbm, osem)


def back(acts, dec, resid, bias, pen):
    dma = pltpu.SemaphoreType.DMA
    vmem = pl.BlockSpec(memory_space=pltpu.VMEM)
    anyspace = pl.BlockSpec(memory_space=pl.ANY)
    return pl.pallas_call(
        back_kernel,
        name="back",
        out_shape=(jax.ShapeDtypeStruct((4, 4, 2, 16, D), BF), jax.ShapeDtypeStruct((8, 128), F32)),
        in_specs=[anyspace, anyspace, vmem, vmem, vmem],
        out_specs=(anyspace, vmem),
        scratch_shapes=[
            pltpu.VMEM((512, 512), BF), pltpu.VMEM((512, D), BF), dma((2,)),
            pltpu.VMEM((3, 2, 4, 4, 4, 16, 384), BF), pltpu.VMEM((3, 4, 4, 4, 16, 384), BF), dma((3, 4)), dma((3, 4)),
            pltpu.VMEM((3, 3, 4, 4, 16, 384), BF), dma((3, 3)), dma((3, 3)),
            pltpu.VMEM((3, 4, 4, 16, 384), BF), pltpu.VMEM((3, 3, 4, 16, 384), BF), dma((3, 3)), dma((3, 3)),
            pltpu.VMEM((3, 4, 16, 384), BF), pltpu.VMEM((3, 3, 16, 384), BF), dma((3, 3)), dma((3, 3)),
            pltpu.VMEM((4, 8, 128), F32), pltpu.VMEM((3, 7, 8, 128), F32), dma((3, 7)), dma((3, 7)),
            pltpu.VMEM((3, 2, 4, 4, 4, 16, 384), BF), dma(()),
        ] + gather_sems(),
        compiler_params=pltpu.CompilerParams(collective_id=1, has_side_effects=True, vmem_limit_bytes=60 << 20),
    )(acts, dec, resid, bias, pen)


def rope_tables():
    j = np.arange(HEAD_DIM // 2, dtype=np.float32)
    frequency = np.power(np.float32(rope_base), np.float32(-2.0) * j / np.float32(HEAD_DIM)).astype(np.float32)
    angles = (np.arange(TOKENS, dtype=np.float32)[:, None] * frequency[None, :]).astype(np.float32)
    cos, sin = np.cos(angles).astype(np.float32), np.sin(angles).astype(np.float32)
    return np.concatenate([cos, cos], 1), np.concatenate([-sin, sin], 1)


def per_device(
    x_in, doc_lengths, attn_gain, w_query, w_key, w_value, w_out, post_gain, enc_weight, enc_bias, dec_weight, dec_bias
):
    tokens = TOKENS
    cos, sin = rope_tables()
    bias4 = dec_bias.reshape(4, 1, 1152)
    resid, gathered = front(
        doc_lengths, attn_gain.reshape(1, 1152), post_gain.reshape(4, 1, 1152), bias4, x_in,
        jnp.asarray(cos), jnp.asarray(sin), w_query, w_key, w_value, w_out,
    )
    centered = gathered.reshape(tokens, D)
    pre_acts = jnp.dot(centered, enc_weight, preferred_element_type=F32) + enc_bias
    latent_acts = jnp.maximum(pre_acts, 0.0).astype(BF)
    row_norms = jnp.sqrt(jnp.sum(jnp.square(dec_weight.astype(F32)), axis=1) + norm_eps)
    act_sums = jnp.sum(latent_acts.astype(F32), axis=0)
    penalty_part = jnp.sum(act_sums * row_norms)
    grad_full, loss = back(latent_acts, dec_weight, resid, bias4, penalty_part.reshape(1, 1))
    grad_recon = grad_full.reshape(tokens, D)
    upstream = lax.dot_general(grad_recon, dec_weight, (((1,), (1,)), ((), ())), preferred_element_type=F32)
    grad_pre = jnp.where(pre_acts > 0, upstream + l1_weight * row_norms / tokens, 0.0).astype(BF)
    grad_enc = lax.dot_general(centered, grad_pre, (((0,), (0,)), ((), ())), preferred_element_type=F32).astype(BF)
    decoder_term = lax.dot_general(latent_acts, grad_recon, (((0,), (0,)), ((), ())), preferred_element_type=F32)
    grad_dec = (
        decoder_term + l1_weight / tokens * act_sums[:, None] * dec_weight.astype(F32) / row_norms[:, None]
    ).astype(BF)
    return (grad_enc, grad_dec, loss[0, 0])


def solution(mesh):
    placed = (
        P(None, "width"),
        P(),
        P("width"),
        P("width", "heads"),
        P("width", "heads"),
        P("width", "heads"),
        P("heads", "width"),
        P(),
        P(None, ("heads", "width", "sae")),
        P(("heads", "width", "sae")),
        P(("heads", "width", "sae"), None),
        P(),
    )
    return jax.shard_map(
        per_device,
        mesh=mesh,
        in_specs=placed,
        out_specs=(P(None, ("heads", "width", "sae")), P(("heads", "width", "sae"), None), P()),
        check_vma=False,
    )
```

time: 472 us -> 154 us (0.33)
  waiting for transfers between devices: 247 us -> 0 us
  blocking collectives: 128 us -> 0 us
  Pallas kernels: 0 us -> 122 us
  other arithmetic: 31.4 us -> 3.97 us
  matrix products: 45.7 us -> 22.9 us
  between operations: 16.5 us -> 0.76 us
    psum x2 -> x0, waiting for transfers between devices: 143 us -> none  [the longest x1 94.4 us: per_device(): recon = lax.psum(recon_part, ('heads', 'width', 'sae')) + dec_bias]
    psum x3 -> x0, blocking collectives: 128 us -> none  [the longest x1 65.8 us: per_device(): penalty_total = lax.psum(penalty_part, ('heads', 'width', 'sae'))]
    pallas_call x0 -> x2, Pallas kernels: none -> 122 us  [the longest x1 62.6 us: back(): pl.pallas_call(back_kernel, name='back', out_shape=(jax.ShapeDtypeStruct(...]
    all_gather x2 -> x0, waiting for transfers between devices: 103 us -> none  [the longest x1 51.8 us: per_device(): lax.all_gather(attn_local, 'width', axis=1, tiled=True)]
    dot_general x8 -> x1, matrix products: 24.5 us -> 7.17 us  [per_device(): jnp.dot(centered, enc_weight, preferred_element_type=F32) + enc_bias]
    reduce_sum x6 -> x1, other arithmetic: 16 us -> 3.36 us  [per_device(): jnp.sum(jnp.square(dec_weight.astype(F32)), axis=1) + norm_eps]
    convert_element_type x2 -> x0, other arithmetic: 5.92 us -> none  [the longest x1 5.92 us: per_device(): (x_full.astype(jnp.float32) + proj_float * inverse_post[:, None] * post_g...]
  transfers between devices with their start and end apart: 4 -> 0, of which waited for: 4 -> 0; matrix products, arithmetic and copies ran while one was open for 2% -> 0% of each run, Pallas kernels for 0% -> 0%
where the time goes in v1:
time: 154 us; the launch traced here: 152 us
  Pallas kernels  122 us (79%)
  matrix products  22.9 us (15%)
  other arithmetic  3.97 us (3%)
  local copies, waits for them, and re-layouts  3.08 us (2%)
    pallas_call x1, Pallas kernels, back(): pl.pallas_call(back_kernel, name='back', out_shape=(jax.ShapeDtypeStruct(...  62.6 us
    pallas_call x1, Pallas kernels, front(): pl.pallas_call(front_kernel, name='front', out_shape=(jax.ShapeDtypeStruc...  59.1 us
    dot_general x1, matrix products, per_device(): jnp.dot(centered, enc_weight, preferred_element_type=F32) + enc_bias  7.17 us
    dot_general x1, matrix products, per_device(): lax.dot_general(grad_recon, dec_weight, (((1,), (1,)), ((), ())), preferr...  6.53 us
    dot_general x1, matrix products, per_device(): lax.dot_general(latent_acts, grad_recon, (((0,), (0,)), ((), ())), prefer...  4.94 us
    dot_general x1, matrix products, per_device(): lax.dot_general(centered, grad_pre, (((0,), (0,)), ((), ())), preferred_e...  4.31 us
    reduce_sum x1, other arithmetic, per_device(): jnp.sum(jnp.square(dec_weight.astype(F32)), axis=1) + norm_eps  3.36 us

profile of v1, /device:TPU:1, one launch (start us, length us, event | category | flops | bytes accessed | tf_op | source)
XLA Modules:
  0.0 152.5 jit_solution(7350748619066988320)
XLA Ops:
  0.6 0.0 copy-start.1
  0.6 0.0 copy-start.5
  0.7 0.0 copy-start.2
  0.7 0.0 copy-start.3
  0.7 3.4 %fusion = f32[512]{0:T(512)S(1)} fusion(bf16[512,4608]{1,0:T(8,128)(2,1)} %dec_hbm.1), kind=kLoop, calls=%fused_computation.2 | loop fusion | flops 7077376 | bytes 4720640 | tf_op jit(solution)/shard_map/reduce_sum | solution.py:427
  4.0 0.0 copy-done.3
  4.0 0.6 reshape.38.gain_ref
  4.6 0.0 copy-done.1
  4.6 0.6 reshape.40.bias_ref
  5.3 0.0 copy-done.2
  5.3 0.6 reshape.39.post_ref
  5.9 59.1 %front.1 = (bf16[16,1152]{1,0:T(8,128)(2,1)}, bf16[4,4,2,16,4608]{4,3,2,1,0:T(8,128)(2,1)}) custom-call(s32[4]{0:T(128)} %doc_ref.1, f32[1,1152]{1,0:T(1,128)} %reshape.38.gain_ref, f32[4,1,1152]{2,1,0:T(1,128)} %reshape.39.post_ref, f32[4,1,1152]{2,1,0:T(1,128)} %reshape.40.bias_ref, bf16[512,1152]{1,0:T(8,128)(2,1)} %x_hbm.1, ...), custom_call_target="tpu_custom_call" | custom-call | tf_op jit(solution)/shard_map/front/pallas_call | solution.py:259
  65.0 0.0 copy-done.5
  65.0 7.2 %convert_reduce_fusion = (f32[512]{0:T(512)S(1)}, bf16[512,512]{1,0:T(8,128)(2,1)}, f32[512,512]{1,0:T(8,128)S(1)}) fusion(f32[512]{0:T(512)S(1)} %copy-done.5, bf16[512,4608]{1,0:T(8,128)(2,1)} %bitcast.14, bf16[4608,512]{1,0:T(8,128)(2,1)} %param.22), kind=kOutput, calls=%fused_computation.11 | convolution fusion | flops 2417229312 | bytes 11014144 | tf_op jit(solution)/shard_map/dot_general | solution.py:425
  72.2 0.6 broadcast_multiply_fusion
  72.8 0.0 slice-start
  72.8 62.6 %back.1 = (bf16[4,4,2,16,4608]{4,3,2,1,0:T(8,128)(2,1)}, f32[8,128]{1,0:T(8,128)}) custom-call(bf16[512,512]{1,0:T(8,128)(2,1)} %get-tuple-element.12.acts_hbm, bf16[512,4608]{1,0:T(8,128)(2,1)} %dec_hbm.1, bf16[16,1152]{1,0:T(8,128)(2,1)} %get-tuple-element.8.resid_ref, f32[4,1,1152]{2,1,0:T(1,128)} %reshape.40.bias_ref, f32[1,1]{1,0:T(1,128)} %bitcast.1.pen_ref), custom_call_target="tpu_custom_call" | custom-call | tf_op jit(solution)/shard_map/back/pallas_call | solution.py:387
  135.4 1.2 slice.3
  136.6 0.0 slice-start.1
  136.6 0.0 copy-start
  136.6 0.0 copy-start.4
  136.6 0.0 slice-start.2
  136.6 6.5 %fusion.5 = bf16[512,512]{1,0:T(8,128)(2,1)S(1)} fusion(bf16[512,4608]{1,0:T(8,128)(2,1)} %bitcast.18, bf16[512,4608]{1,0:T(8,128)(2,1)} %dec_hbm.1, f32[512,512]{1,0:T(8,128)S(1)} %get-tuple-element.17, f32[512]{0:T(512)S(1)} %get-tuple-element.16), kind=kOutput, calls=%fused_computation.10 | convolution fusion | flops 2416967680 | bytes 11012096 | tf_op jit(solution)/shard_map/dot_general | solution.py:432
  143.2 0.0 slice-done
  143.2 0.0 slice-done.1
  143.2 0.0 copy-done
  143.2 0.0 copy-done.4
  143.2 0.0 slice-start.3
  143.2 4.9 %fusion.3 = bf16[512,4608]{1,0:T(8,128)(2,1)} fusion(bf16[512,4608]{1,0:T(8,128)(2,1)S(1)} %bitcast.13, bf16[512,512]{1,0:T(8,128)(2,1)S(1)} %copy-done, bf16[512,4608]{1,0:T(8,128)(2,1)S(1)} %bitcast.19, f32[512]{0:T(512)S(1)} %get-tuple-element.15, f32[512]{0:T(512)S(1)} %get-tuple-element.13), kind=kOutput, calls=%fused_computation.5 | convolution fusion | flops 2427715584 | bytes 14684160 | tf_op jit(solution)/shard_map/dot_general | solution.py:435
  148.2 0.0 slice-done.2
  148.2 0.0 slice-done.3
  148.2 4.3 %convolution_convert_fusion = bf16[4608,512]{1,0:T(8,128)(2,1)} fusion(bf16[512,4608]{1,0:T(8,128)(2,1)S(1)} %bitcast.17, bf16[512,512]{1,0:T(8,128)(2,1)S(1)} %fusion.5), kind=kOutput, calls=%fused_computation.6 | convolution fusion | flops 2418278400 | bytes 9961472 | tf_op jit(solution)/shard_map/dot_general | solution.py:434
  (2 shorter events, 0.0 us)
Async XLA Ops:
  0.6 4.0 %copy-start.1 = (f32[4608]{0:T(1024)S(1)}, f32[4608]{0:T(1024)}, u32[]{:S(2)}) copy-start(f32[4608]{0:T(1024)} %param.25) | copy-start | bytes 55300
  0.6 64.3 %copy-start.5 = (f32[512]{0:T(512)S(1)}, f32[512]{0:T(512)}, u32[]{:S(2)}) copy-start(f32[512]{0:T(512)} %param.23) | copy-start | bytes 6148
  0.7 4.6 %copy-start.2 = (f32[4608]{0:T(1024)S(1)}, f32[4608]{0:T(1024)}, u32[]{:S(2)}) copy-start(f32[4608]{0:T(1024)} %param.21) | copy-start | bytes 55300
  0.7 3.4 %copy-start.3 = (f32[1152]{0:T(1024)S(1)}, f32[1152]{0:T(1024)}, u32[]{:S(2)}) copy-start(f32[1152]{0:T(1024)} %param.16) | copy-start | bytes 13828
  72.8 70.4 %slice-start = ((s8[4718592]{0:T(1024)(128)(4,1)}), s8[524288]{0:T(1024)(128)(4,1)S(1)}, s32[]{:S(2)}) async-start(s8[4718592]{0:T(1024)(128)(4,1)} %bitcast.12), calls=%async_computation | async-start | bytes 1048576
  136.6 6.6 %slice-start.1 = ((s8[4718592]{0:T(1024)(128)(4,1)}), s8[4194304]{0:T(1024)(128)(4,1)S(1)}, s32[]{:S(2)}) async-start(s8[4718592]{0:T(1024)(128)(4,1)} %bitcast.12), calls=%async_computation.1 | async-start | bytes 8388608
  136.6 6.6 %copy-start = (bf16[512,512]{1,0:T(8,128)(2,1)S(1)}, bf16[512,512]{1,0:T(8,128)(2,1)}, u32[]{:S(2)}) copy-start(bf16[512,512]{1,0:T(8,128)(2,1)} %get-tuple-element.12.acts_hbm) | copy-start | bytes 1572868
  136.6 6.6 %copy-start.4 = (bf16[4,4,2,16,4608]{4,3,2,1,0:T(8,128)(2,1)S(1)}, bf16[4,4,2,16,4608]{4,3,2,1,0:T(8,128)(2,1)}, u32[]{:S(2)}) copy-start(bf16[4,4,2,16,4608]{4,3,2,1,0:T(8,128)(2,1)} %get-tuple-element.9) | copy-start | bytes 14155780
  136.6 11.5 %slice-start.2 = ((s8[4718592]{0:T(1024)(128)(4,1)}), s8[4194304]{0:T(1024)(128)(4,1)S(1)}, s32[]{:S(2)}) async-start(s8[4718592]{0:T(1024)(128)(4,1)} %bitcast.15), calls=%async_computation.2 | async-start | bytes 8388608
  143.2 5.0 %slice-start.3 = ((s8[4718592]{0:T(1024)(128)(4,1)}), s8[524288]{0:T(1024)(128)(4,1)S(1)}, s32[]{:S(2)}) async-start(s8[4718592]{0:T(1024)(128)(4,1)} %bitcast.15), calls=%async_computation.3 | async-start | bytes 1048576

commit v2 on v1

v2 whole, which is shorter than its diff:
```python
import functools

import jax
import jax.numpy as jnp
import numpy as np
from jax import lax
from jax.experimental import pallas as pl
from jax.experimental.pallas import tpu as pltpu
from jax.sharding import PartitionSpec as P

D = 4608
HEADS = 32
HEAD_DIM = 128
TOKENS = 512

norm_eps = 1e-06
soft_cap = 50.0
rope_base = 10000.0
l1_weight = 3.0

MESH = pl.DeviceIdType.MESH
BF = jnp.bfloat16
F32 = jnp.float32
HIGHEST = lax.Precision.HIGHEST

ORDERS = (("y", "x", "z"), ("x", "z", "y"), ("z", "y", "x"))


class Nav:
    def __init__(self):
        self.h = lax.axis_index("heads")
        self.y = lax.axis_index("width")
        self.x = lax.axis_index("sae")
        self.z = self.h // 2
        self.c = self.h % 2

    def index(self, axis):
        return {"x": self.x, "y": self.y, "z": self.z}[axis]

    def peer(self, axis, d):
        if axis == "c":
            return {"heads": self.z * 2 + (1 - self.c)}
        if axis == "h":
            return {"heads": (self.h + d) % 8}
        if axis == "z":
            return {"heads": ((self.z + d) % 4) * 2 + self.c}
        if axis == "y":
            return {"width": (self.y + d) % 4}
        return {"sae": (self.x + d) % 4}


def send(src, dst, ssem, rsem, device):
    copy = pltpu.make_async_remote_copy(
        src_ref=src, dst_ref=dst, send_sem=ssem, recv_sem=rsem, device_id=device, device_id_type=MESH
    )
    copy.start()
    return copy


def barrier(nav):
    sem = pltpu.get_barrier_semaphore()
    peers = [("h", d) for d in range(1, 8)] + [(a, d) for a in "xy" for d in (1, 2, 3)]
    for axis, d in peers:
        pl.semaphore_signal(sem, inc=1, device_id=nav.peer(axis, d), device_id_type=MESH)
    pl.semaphore_wait(sem, len(peers))


def gather_sems():
    dma = pltpu.SemaphoreType.DMA
    return [dma((3, 3)), dma((3, 3)), dma((3, 3)), dma((3, 3)), dma((3, 4, 3)), dma((3, 4, 3)), dma((3, 4, 4)), dma((3, 4, 4))]


def all_gather(nav, full, sems, filler, unit):
    s1, r1, s2, r2, s3, r3, sc, rc = sems
    c = nav.c
    first, second, third, core = {}, {}, {}, {}
    place = [[nav.index(a) for a in order] for order in ORDERS]

    def share(p, d, e):
        part = full.at[p, c, (place[p][2] + 4 - d) % 4, (place[p][1] + 4 - e) % 4]
        core[p, d, e] = send(part, part, sc.at[p, d, e], rc.at[p, d, e], nav.peer("c", 1))

    def spread(p, e):
        part = full.at[p, c, place[p][2], (place[p][1] + 4 - e) % 4]
        for d in (2, 1, 3):
            third[p, e, d] = send(part, part, s3.at[p, e, d - 1], r3.at[p, e, d - 1], nav.peer(ORDERS[p][2], d))
        share(p, 0, e)

    def collect(d):
        for e in (0, 1, 3, 2):
            for p in range(3):
                third[p, e, d].wait_recv()
                share(p, d, e)

    def units(d):
        for p in range(3):
            for e in range(4):
                core[p, d, e].wait_recv()
            unit(p, (place[p][2] + 4 - d) % 4)

    for p, order in enumerate(ORDERS):
        i1, i2, i3 = place[p]
        block = full.at[p, c, i3, i2, i1]
        for d in (2, 1, 3):
            first[p, d] = send(block, block, s1.at[p, d - 1], r1.at[p, d - 1], nav.peer(order[0], d))
    filler(0)
    for p, order in enumerate(ORDERS):
        i1, i2, i3 = place[p]
        for d in (1, 2, 3):
            first[p, d].wait_recv()
        part = full.at[p, c, i3, i2]
        for d in (2, 1, 3):
            second[p, d] = send(part, part, s2.at[p, d - 1], r2.at[p, d - 1], nav.peer(order[1], d))
        spread(p, 0)
    filler(1)
    for e in (1, 3, 2):
        for p in range(3):
            second[p, e].wait_recv()
            spread(p, e)
    filler(2)
    units(0)
    collect(1)
    collect(3)
    units(1)
    collect(2)
    units(3)
    units(2)
    for group in (first, second, third, core):
        for copy in group.values():
            copy.wait_send()


def columns(w, p):
    start = w * 1152 + p * 384
    if isinstance(start, int):
        return slice(start, start + 384)
    return pl.ds(pl.multiple_of(start, 128), 384)


def slab_rows(p, k3):
    if p == 0:
        return (slice(None), k3)
    if p == 1:
        return ()
    return (slice(None), slice(None), k3)


def slab_pieces(p, k3):
    if p == 1:
        return [((1, slice(None), k3), k3)]
    if p == 0:
        return [((0, slice(None), k3, slice(None), w), w) for w in range(4)]
    return [((2, slice(None), k3, w), w) for w in range(4)]


def unpack(full, out, sem, p, k3):
    for idx, w in slab_pieces(p, k3):
        rows = slab_rows(p, k3)
        rows = rows + (slice(None),) * (4 - len(rows))
        pltpu.make_async_copy(full.at[idx], out.at[rows + (columns(w, p),)], sem).start()


def flat(t):
    return t.reshape(-1, t.shape[-1])


def row_of(ref, y=None):
    n = ref.shape[0]
    if y is None:
        return jnp.concatenate([ref[j : j + 1] for j in range(n)], axis=1)
    q = n // 4
    rows = []
    for j in range(q):
        t = ref[j : j + 1]
        for k in range(1, 4):
            t = jnp.where(y == k, ref[k * q + j : k * q + j + 1], t)
        rows.append(t)
    return jnp.concatenate(rows, axis=1)


def front(nav, doc_ref, gain_ref, post_ref, bias_row, loads, refs):
    (xv, cosv, sinv, wq, wk, wv, wo, part32, part16, got1, ss1, got_ss, s1, r1, s1b, r1b,
     kv, s3, r3, mixed, s5, r5, proj, got7, s7, r7, sq8, got8, s8, r8) = refs
    h, y, x = nav.h, nav.y, nav.x
    loads["x"].wait()
    xf = xv[...].astype(F32)
    ss1[...] = lax.dot_general(
        jnp.ones((8, 1152), F32), xf * xf, (((1,), (1,)), ((), ())), precision=HIGHEST, preferred_element_type=F32
    )
    square = [send(ss1, got_ss.at[d - 1], s1b.at[d - 1], r1b.at[d - 1], nav.peer("y", d)) for d in (1, 2, 3)]
    scaled = (xf * row_of(gain_ref)).astype(BF)
    for name in ("q", "k", "v"):
        loads[name].wait()
    for kvh in range(2):
        cols = slice(kvh * 128, kvh * 128 + 128)
        key = jnp.dot(scaled, wk[:, cols], preferred_element_type=F32)
        val = jnp.dot(scaled, wv[:, cols], preferred_element_type=F32)
        for g in range(2):
            w = kvh * 2 + g
            q = jnp.dot(scaled, wq[:, w * 128 : w * 128 + 128], preferred_element_type=F32)
            for k, t in enumerate((q, key, val)):
                part32[w, :, k * 128 : k * 128 + 128] = t
                part16[w, :, k * 128 : k * 128 + 128] = t.astype(BF)
    moved = [send(part16.at[(y + d) % 4], got1.at[d - 1], s1.at[d - 1], r1.at[d - 1], nav.peer("y", d)) for d in (2, 1, 3)]
    bounds = []
    run = 0
    for j in range(4):
        run = run + doc_ref[j]
        bounds.append(run)
    qpos = x * 128 + lax.broadcasted_iota(jnp.int32, (128, 512), 0)
    kpos = lax.broadcasted_iota(jnp.int32, (128, 512), 1)
    qseg = sum((b <= qpos).astype(jnp.int32) for b in bounds)
    kseg = sum((b <= kpos).astype(jnp.int32) for b in bounds)
    allowed = (qseg == kseg) & (kpos <= qpos)
    for copy in square:
        copy.wait_recv()
    total = ss1[...] + got_ss[0] + got_ss[1] + got_ss[2]
    spread = lax.dot_general(
        total, jnp.full((8, 128), 0.125, F32), (((0,), (0,)), ((), ())), precision=HIGHEST, preferred_element_type=F32
    )
    inverse = lax.rsqrt(spread / D + norm_eps)
    loads["cos"].wait()
    loads["sin"].wait()
    for copy in moved:
        copy.wait_recv()
    qkv = []
    for k in range(3):
        cols = slice(k * 128, k * 128 + 128)
        t = part32[y, :, cols] + got1[0, :, cols].astype(F32) + got1[1, :, cols].astype(F32) + got1[2, :, cols].astype(F32)
        t = t * inverse
        if k < 2:
            t = t * cosv[...] + pltpu.roll(t, 64, 1) * sinv[...]
        qkv.append(t.astype(BF))
    kv[x, :, 0:128] = qkv[1]
    kv[x, :, 128:256] = qkv[2]
    spreads = [send(kv.at[x], kv.at[x], s3.at[d - 1], r3.at[d - 1], nav.peer("x", d)) for d in (2, 1, 3)]
    for copy in spreads:
        copy.wait_recv()
    keys = kv[:, :, 0:128].reshape(512, 128)
    vals = kv[:, :, 128:256].reshape(512, 128)
    scores = lax.dot_general(qkv[0], keys, (((1,), (1,)), ((), ())), preferred_element_type=F32) * ((D // HEADS) ** -0.5)
    capped = soft_cap * jnp.tanh(scores / soft_cap)
    weights = jnp.where(allowed, jnp.exp(capped), 0.0)
    probs = (weights / jnp.sum(weights, axis=-1, keepdims=True)).astype(BF)
    mixed[y] = jnp.dot(probs, vals, preferred_element_type=F32).astype(BF)
    mixes = [send(mixed.at[y], mixed.at[y], s5.at[d - 1], r5.at[d - 1], nav.peer("y", d)) for d in (2, 1, 3)]
    loads["o"].wait()
    for copy in mixes:
        copy.wait_recv()
    whole = jnp.concatenate([mixed[w] for w in range(4)], axis=1)
    for k in range(3):
        cols = slice(k * 384, k * 384 + 384)
        t = jnp.dot(whole, wo[:, cols], preferred_element_type=F32).astype(BF)
        proj[:, :, cols] = t.reshape(8, 16, 384)
    parts = [send(proj.at[(h + d) % 8], got7.at[d - 1], s7.at[d - 1], r7.at[d - 1], nav.peer("h", d)) for d in range(1, 8)]
    for copy in parts:
        copy.wait_recv()
    acc = proj[h].astype(F32)
    for d in range(7):
        acc = acc + got7[d].astype(F32)
    acc = acc.astype(BF).astype(F32)
    sq8[...] = jnp.broadcast_to(jnp.sum(acc * acc, axis=1, keepdims=True), (16, 128))
    norms = [send(sq8, got8.at[d - 1], s8.at[d - 1], r8.at[d - 1], nav.peer("y", d)) for d in (2, 1, 3)]
    for copy in norms:
        copy.wait_recv()
    inverse_post = lax.rsqrt((sq8[...] + got8[0] + got8[1] + got8[2]) / D + norm_eps)[:, 0:1]
    own_x = xv[pl.ds(pl.multiple_of(h * 16, 16), 16), :].astype(F32)
    resid = (own_x + acc * inverse_post * row_of(post_ref, y)).astype(BF)
    centered = (resid.astype(F32) - bias_row).astype(BF)
    sends = square + moved + spreads + mixes + parts + norms
    return resid, centered, sends


def step_kernel(
    doc_ref, gain_ref, post_ref, bias_ref, ebias_ref, x_hbm, cos_hbm, sin_hbm, wq_hbm, wk_hbm, wv_hbm, wo_hbm,
    enc_hbm, dec_hbm,
    cent_hbm, grad_hbm, acts_ref, gpre_ref, coef_ref, loss_ref,
    enc, dec, lsem, osem, resid_ref, full, pre, norms, norm_row,
    part, got0, s0, r0, got3, s3, r3, slab, got2, s2, r2, strip, got1, s1, r1,
    pool_h, pool_y, pool_x, sl, rl, gfull, *rest,
):
    fsems, gsems, frefs = rest[:8], rest[8:16], rest[16:]
    nav = Nav()
    c, h, y, x = nav.c, nav.h, nav.y, nav.x
    place = [[nav.index(a) for a in order] for order in ORDERS]
    rows = pl.ds(pl.multiple_of(x * 128, 128), 128)
    xv, cosv, sinv, wq, wk, wv, wo = frefs[:7]
    loads = {}
    for k, (name, src, dst) in enumerate([
        ("x", x_hbm.at[rows], xv), ("q", wq_hbm, wq), ("k", wk_hbm, wk), ("v", wv_hbm, wv),
        ("cos", cos_hbm.at[rows], cosv), ("sin", sin_hbm.at[rows], sinv), ("o", wo_hbm, wo),
        ("dec", dec_hbm, dec), ("enc", enc_hbm, enc),
    ]):
        loads[name] = pltpu.make_async_copy(src, dst, lsem.at[k])
        loads[name].start()
    barrier(nav)
    bias_row = row_of(bias_ref, y)
    resid, centered, sends = front(nav, doc_ref, gain_ref, post_ref, bias_row, loads, frefs[:-1])
    resid_ref[...] = resid
    for p in range(3):
        i1, i2, i3 = place[p]
        full[p, c, i3, i2, i1] = centered[:, p * 384 : p * 384 + 384]

    def norms_filler(k):
        if k == 0:
            loads["dec"].wait()
            loads["enc"].wait()

            def body(j, carry):
                r = pl.ds(pl.multiple_of(j * 32, 32), 32)
                t = jnp.zeros((32, 128), F32)
                for m in range(36):
                    v = dec[r, m * 128 : m * 128 + 128].astype(F32)
                    t = t + v * v
                norms[r, :] = t
                return carry

            lax.fori_loop(0, 16, body, 0)
            pre[...] = jnp.zeros(pre.shape, F32)
        if k == 1:
            sums = lax.dot_general(
                jnp.ones((8, 128), F32), norms[...], (((1,), (1,)), ((), ())), precision=HIGHEST, preferred_element_type=F32
            )
            norm_row[...] = jnp.sqrt(sums + norm_eps)

    def encode(p, k3):
        dst = slab_rows(p, k3) + (Ellipsis,)
        t = pre[dst]
        shape = t.shape
        t = flat(t)
        for idx, w in slab_pieces(p, k3):
            t = t + jnp.dot(flat(full[idx]), enc[columns(w, p), :], preferred_element_type=F32)
        pre[dst] = t.reshape(shape)
        unpack(full, cent_hbm, osem.at[0], p, k3)

    all_gather(nav, full, fsems, norms_filler, encode)
    act_sum = jnp.zeros((1, 512), F32)
    ebias = row_of(ebias_ref)
    for k in range(2):
        t = flat(pre[k]) + ebias
        pre[k] = t.reshape(4, 4, 16, 512)
        acts = jnp.maximum(t, 0.0).astype(BF)
        acts_ref[k] = acts.reshape(4, 4, 16, 512)
        act_sum = act_sum + jnp.sum(acts.astype(F32), axis=0, keepdims=True)
    penalty = jnp.sum(act_sum * norm_row[0:1], keepdims=True)
    coef_ref[...] = (l1_weight / TOKENS) * act_sum / norm_row[...]

    swap, third, second, first = {}, {}, {}, {}

    def produce(p, d):
        t3 = (place[p][2] + d) % 4
        left = flat(acts_ref[slab_rows(p, t3) + (Ellipsis,)])
        for idx, w in slab_pieces(p, t3):
            t = jnp.dot(left, dec[:, columns(w, p)], preferred_element_type=F32).astype(BF)
            part[idx] = t.reshape((2, 4, 4, 16, 384) if p == 1 else (2, 4, 16, 384))
        swap[p, d] = send(part.at[p, 1 - c, t3], got0.at[p, t3], s0.at[p, d], r0.at[p, d], nav.peer("c", 1))

    def combine(p, d):
        t3 = (place[p][2] + d) % 4
        swap[p, d].wait_recv()
        if d:
            part[p, c, t3] = (part[p, c, t3].astype(F32) + got0[p, t3].astype(F32)).astype(BF)
            third[p, d] = send(part.at[p, c, t3], got3.at[p, d - 1], s3.at[p, d - 1], r3.at[p, d - 1], nav.peer(ORDERS[p][2], d))

    order = [(p, d) for d in (2, 1, 3, 0) for p in (1, 0, 2)]
    for k, (p, d) in enumerate(order):
        produce(p, d)
        if k:
            combine(*order[k - 1])
    combine(*order[-1])
    for p in range(3):
        i1, i2, i3 = place[p]
        for d in (1, 2, 3):
            third[p, d].wait_recv()
        t = part[p, c, i3].astype(F32) + got0[p, i3].astype(F32)
        for d in range(3):
            t = t + got3[p, d].astype(F32)
        slab[p] = t.astype(BF)
        for d in (2, 1, 3):
            second[p, d] = send(slab.at[p, (i2 + d) % 4], got2.at[p, d - 1], s2.at[p, d - 1], r2.at[p, d - 1], nav.peer(ORDERS[p][1], d))
    for p in range(3):
        i1, i2, i3 = place[p]
        for d in (1, 2, 3):
            second[p, d].wait_recv()
        t = slab[p, i2].astype(F32)
        for d in range(3):
            t = t + got2[p, d].astype(F32)
        strip[p] = t.astype(BF)
        for d in (2, 1, 3):
            first[p, d] = send(strip.at[p, (i1 + d) % 4], got1.at[p, d - 1], s1.at[p, d - 1], r1.at[p, d - 1], nav.peer(ORDERS[p][0], d))
    squares = jnp.zeros((16, 384), F32)
    for p in range(3):
        i1, i2, i3 = place[p]
        cols = slice(p * 384, p * 384 + 384)
        for d in (1, 2, 3):
            first[p, d].wait_recv()
        t = strip[p, i1].astype(F32)
        for d in range(3):
            t = t + got1[p, d].astype(F32)
        error = t + bias_row[:, cols] - resid_ref[:, cols].astype(F32)
        squares = squares + error * error
        gfull[p, c, i3, i2, i1] = (2.0 / TOKENS * error).astype(BF)

    pools = [(pool_h, "h", 8, h), (pool_y, "y", 4, y), (pool_x, "x", 4, x)]
    losses = []

    def pool_send(k):
        pool, axis, n, me = pools[k]
        for d in range(1, n):
            losses.append(send(pool.at[me], pool.at[me], sl.at[k, d - 1], rl.at[k, d - 1], nav.peer(axis, d)))

    def pool_sum(k):
        pool, axis, n, me = pools[k]
        for copy in losses[-(n - 1) :]:
            copy.wait_recv()
        total = pool[0]
        for j in range(1, n):
            total = total + pool[j]
        return total

    def loss_filler(k):
        if k == 0:
            pool_h[h] = jnp.broadcast_to(jnp.sum(squares, keepdims=True), (8, 128)) + l1_weight * penalty
            pool_send(0)
        if k == 1:
            pool_y[y] = pool_sum(0)
            pool_send(1)
        if k == 2:
            pool_x[x] = pool_sum(1)
            pool_send(2)

    upstream = frefs[-1]
    upstream[...] = jnp.zeros(upstream.shape, F32)

    def decode(p, k3):
        dst = slab_rows(p, k3) + (Ellipsis,)
        t = upstream[dst]
        shape = t.shape
        t = flat(t)
        for idx, w in slab_pieces(p, k3):
            t = t + lax.dot_general(
                flat(gfull[idx]), dec[:, columns(w, p)], (((1,), (1,)), ((), ())), preferred_element_type=F32
            )
        upstream[dst] = t.reshape(shape)
        unpack(gfull, grad_hbm, osem.at[1], p, k3)

    all_gather(nav, gfull, gsems, loss_filler, decode)
    loss_ref[...] = pool_sum(2) / (TOKENS * D)
    lift = (l1_weight / TOKENS) * norm_row[0:1]
    for k in range(2):
        t = jnp.where(flat(pre[k]) > 0, flat(upstream[k]) + lift, 0.0).astype(BF)
        gpre_ref[k] = t.reshape(4, 4, 16, 512)
    for group in (swap, third, second, first):
        for copy in group.values():
            copy.wait_send()
    for copy in losses + sends:
        copy.wait_send()
    pltpu.make_async_copy(cent_hbm, cent_hbm, osem.at[0]).wait()
    pltpu.make_async_copy(grad_hbm, grad_hbm, osem.at[1]).wait()


def step(*args):
    dma = pltpu.SemaphoreType.DMA
    vmem = pl.BlockSpec(memory_space=pltpu.VMEM)
    anyspace = pl.BlockSpec(memory_space=pl.ANY)
    V = pltpu.VMEM
    front_scratch = [
        V((128, 1152), BF), V((128, 128), F32), V((128, 128), F32),
        V((1152, 512), BF), V((1152, 256), BF), V((1152, 256), BF), V((512, 1152), BF),
        V((4, 128, 384), F32), V((4, 128, 384), BF), V((3, 128, 384), BF),
        V((8, 128), F32), V((3, 8, 128), F32), dma((3,)), dma((3,)), dma((3,)), dma((3,)),
        V((4, 128, 256), BF), dma((3,)), dma((3,)),
        V((4, 128, 128), BF), dma((3,)), dma((3,)),
        V((8, 16, 1152), BF), V((7, 16, 1152), BF), dma((7,)), dma((7,)),
        V((16, 128), F32), V((3, 16, 128), F32), dma((3,)), dma((3,)),
    ]
    return pl.pallas_call(
        step_kernel,
        name="step",
        out_shape=(
            jax.ShapeDtypeStruct((2, 4, 4, 16, D), BF), jax.ShapeDtypeStruct((2, 4, 4, 16, D), BF),
            jax.ShapeDtypeStruct((2, 4, 4, 16, 512), BF), jax.ShapeDtypeStruct((2, 4, 4, 16, 512), BF),
            jax.ShapeDtypeStruct((8, 512), F32), jax.ShapeDtypeStruct((8, 128), F32),
        ),
        in_specs=[pl.BlockSpec(memory_space=pltpu.SMEM)] + [vmem] * 4 + [anyspace] * 9,
        out_specs=(anyspace, anyspace, vmem, vmem, vmem, vmem),
        scratch_shapes=[
            V((D, 512), BF), V((512, D), BF), dma((9,)), dma((2,)), V((16, 1152), BF),
            V((3, 2, 4, 4, 4, 16, 384), BF), V((2, 4, 4, 16, 512), F32), V((512, 128), F32), V((8, 512), F32),
            V((3, 2, 4, 4, 4, 16, 384), BF), V((3, 4, 4, 4, 16, 384), BF), dma((3, 4)), dma((3, 4)),
            V((3, 3, 4, 4, 16, 384), BF), dma((3, 3)), dma((3, 3)),
            V((3, 4, 4, 16, 384), BF), V((3, 3, 4, 16, 384), BF), dma((3, 3)), dma((3, 3)),
            V((3, 4, 16, 384), BF), V((3, 3, 16, 384), BF), dma((3, 3)), dma((3, 3)),
            V((8, 8, 128), F32), V((4, 8, 128), F32), V((4, 8, 128), F32), dma((3, 7)), dma((3, 7)),
            V((3, 2, 4, 4, 4, 16, 384), BF),
        ] + gather_sems() + gather_sems() + front_scratch + [V((2, 4, 4, 16, 512), F32)],
        compiler_params=pltpu.CompilerParams(collective_id=0, has_side_effects=True, vmem_limit_bytes=60 << 20),
    )(*args)


def rope_tables():
    j = np.arange(HEAD_DIM // 2, dtype=np.float32)
    frequency = np.power(np.float32(rope_base), np.float32(-2.0) * j / np.float32(HEAD_DIM)).astype(np.float32)
    angles = (np.arange(TOKENS, dtype=np.float32)[:, None] * frequency[None, :]).astype(np.float32)
    cos, sin = np.cos(angles).astype(np.float32), np.sin(angles).astype(np.float32)
    return np.concatenate([cos, cos], 1), np.concatenate([-sin, sin], 1)


def per_device(
    x_in, doc_lengths, attn_gain, w_query, w_key, w_value, w_out, post_gain, enc_weight, enc_bias, dec_weight, dec_bias
):
    cos, sin = rope_tables()
    centered, grad_recon, acts, grad_pre, coef, loss = step(
        doc_lengths, attn_gain.reshape(9, 128), post_gain.reshape(36, 128), dec_bias.reshape(36, 128),
        enc_bias.reshape(4, 128), x_in, jnp.asarray(cos), jnp.asarray(sin),
        w_query, w_key, w_value, w_out, enc_weight, dec_weight,
    )
    centered, grad_recon = centered.reshape(TOKENS, D), grad_recon.reshape(TOKENS, D)
    acts, grad_pre = acts.reshape(TOKENS, 512), grad_pre.reshape(TOKENS, 512)
    grad_enc = lax.dot_general(centered, grad_pre, (((0,), (0,)), ((), ())), preferred_element_type=F32).astype(BF)
    decoder_term = lax.dot_general(acts, grad_recon, (((0,), (0,)), ((), ())), preferred_element_type=F32)
    grad_dec = (decoder_term + coef[0][:, None] * dec_weight.astype(F32)).astype(BF)
    return (grad_enc, grad_dec, loss[0, 0])


def solution(mesh):
    placed = (
        P(None, "width"),
        P(),
        P("width"),
        P("width", "heads"),
        P("width", "heads"),
        P("width", "heads"),
        P("heads", "width"),
        P(),
        P(None, ("heads", "width", "sae")),
        P(("heads", "width", "sae")),
        P(("heads", "width", "sae"), None),
        P(),
    )
    return jax.shard_map(
        per_device,
        mesh=mesh,
        in_specs=placed,
        out_specs=(P(None, ("heads", "width", "sae")), P(("heads", "width", "sae"), None), P()),
        check_vma=False,
    )
```

time: 154 us -> 128 us (0.83)
  Pallas kernels: 122 us -> 112 us
  matrix products: 22.9 us -> 13.3 us
  other arithmetic: 3.97 us -> 0 us
    pallas_call x2 -> x1, Pallas kernels: 122 us -> 112 us  [step(): pl.pallas_call(step_kernel, name='step', out_shape=(jax.ShapeDtypeStruct(...]
    dot_general x3 -> x1, matrix products: 18.6 us -> 9 us  [per_device(): lax.dot_general(acts, grad_recon, (((0,), (0,)), ((), ())), preferred_ele...]
    reduce_sum x1 -> x0, other arithmetic: 3.36 us -> none  [per_device(): jnp.sum(jnp.square(dec_weight.astype(F32)), axis=1) + norm_eps]
    reshape x3 -> x0, local copies, waits for them, and re-layouts: 1.84 us -> none  [the longest x1 0.62 us: per_device(): bias4 = dec_bias.reshape(4, 1, 1152)]
where the time goes in v2:
time: 128 us; the launch traced here: 127 us
  Pallas kernels  112 us (88%)
  matrix products  13.3 us (10%)
  local copies, waits for them, and re-layouts  1.91 us (1%)
    pallas_call x1, Pallas kernels, step(): pl.pallas_call(step_kernel, name='step', out_shape=(jax.ShapeDtypeStruct(...  112 us
    dot_general x1, matrix products, per_device(): lax.dot_general(acts, grad_recon, (((0,), (0,)), ((), ())), preferred_ele...  9 us
    dot_general x1, matrix products, per_device(): lax.dot_general(centered, grad_pre, (((0,), (0,)), ((), ())), preferred_e...  4.29 us

profile of v2, /device:TPU:1, one launch (start us, length us, event | category | flops | bytes accessed | tf_op | source)
XLA Modules:
  0.0 127.4 jit_solution(16017843057992186896)
XLA Ops:
  0.6 111.5 %step.1 = (bf16[2,4,4,16,4608]{4,3,2,1,0:T(8,128)(2,1)}, bf16[2,4,4,16,4608]{4,3,2,1,0:T(8,128)(2,1)}, bf16[2,4,4,16,512]{4,3,2,1,0:T(8,128)(2,1)}, bf16[2,4,4,1...) custom-call(s32[4]{0:T(128)} %doc_ref.1, f32[9,128]{1,0:T(8,128)} %bitcast.23, f32[36,128]{1,0:T(8,128)} %bitcast.21, ...), custom_call_target="tpu_custom_call" | custom-call | tf_op jit(solution)/shard_map/step/pallas_call | solution.py:477
  112.1 0.7 slice.6
  112.9 0.0 copy-start
  112.9 0.0 copy-start.1
  112.9 9.0 %fusion = bf16[512,4608]{1,0:T(8,128)(2,1)} fusion(bf16[512,4608]{1,0:T(8,128)(2,1)} %dec_hbm.1, bf16[2,4,4,16,512]{4,3,2,1,0:T(8,128)(2,1)} %get-tuple-element.11, bf16[2,4,4,16,4608]{4,3,2,1,0:T(8,128)(2,1)} %get-tuple-element.12, f32[512]{0:T(512)S(1)} %bitcast.20), kind=kOutput, calls=%fused_computation.1 | convolution fusion | flops 2425356288 | bytes 14682112 | tf_op jit(solution)/shard_map/dot_general | solution.py:521
  121.9 0.0 copy-done
  121.9 0.0 copy-done.1
  121.9 4.3 %bitcast_convert_fusion = bf16[4608,512]{1,0:T(8,128)(2,1)} fusion(bf16[2,4,4,16,4608]{4,3,2,1,0:T(8,128)(2,1)S(1)} %copy-done, bf16[2,4,4,16,512]{4,3,2,1,0:T(8,128)(2,1)S(1)} %copy-done.1), kind=kOutput, calls=%fused_computation.2 | convolution fusion | flops 2418278400 | bytes 9961472 | tf_op jit(solution)/shard_map/dot_general | solution.py:520
  126.2 1.2 slice.7
Async XLA Ops:
  112.9 9.0 %copy-start = (bf16[2,4,4,16,4608]{4,3,2,1,0:T(8,128)(2,1)S(1)}, bf16[2,4,4,16,4608]{4,3,2,1,0:T(8,128)(2,1)}, u32[]{:S(2)}) copy-start(bf16[2,4,4,16,4608]{4,3,2,1,0:T(8,128)(2,1)} %get-tuple-element.9) | copy-start | bytes 14155780
  112.9 9.0 %copy-start.1 = (bf16[2,4,4,16,512]{4,3,2,1,0:T(8,128)(2,1)S(1)}, bf16[2,4,4,16,512]{4,3,2,1,0:T(8,128)(2,1)}, u32[]{:S(2)}) copy-start(bf16[2,4,4,16,512]{4,3,2,1,0:T(8,128)(2,1)} %get-tuple-element.10) | copy-start | bytes 1572868

commit v3 on v2

--- a/solution.py
+++ b/solution.py
@@ -57,17 +57,23 @@
     return copy
 
 
-def barrier(nav):
+def drained(ref, ssem, rsem, device):
+    pltpu.make_async_remote_copy(
+        src_ref=ref, dst_ref=ref, send_sem=ssem, recv_sem=rsem, device_id=device, device_id_type=MESH
+    ).wait_send()
+
+
+def greet(nav):
     sem = pltpu.get_barrier_semaphore()
     peers = [("h", d) for d in range(1, 8)] + [(a, d) for a in "xy" for d in (1, 2, 3)]
     for axis, d in peers:
         pl.semaphore_signal(sem, inc=1, device_id=nav.peer(axis, d), device_id_type=MESH)
-    pl.semaphore_wait(sem, len(peers))
+    return lambda: pl.semaphore_wait(sem, len(peers))
 
 
 def gather_sems():
     dma = pltpu.SemaphoreType.DMA
-    return [dma((3, 3)), dma((3, 3)), dma((3, 3)), dma((3, 3)), dma((3, 4, 3)), dma((3, 4, 3)), dma((3, 4, 4)), dma((3, 4, 4))]
+    return [dma((3,)), dma((3, 3)), dma((3,)), dma((3, 3)), dma((3,)), dma((3, 4, 3)), dma((3,)), dma((3, 4, 4))]
 
 
 def all_gather(nav, full, sems, filler, unit):
@@ -78,56 +84,74 @@
 
     def share(p, d, e):
         part = full.at[p, c, (place[p][2] + 4 - d) % 4, (place[p][1] + 4 - e) % 4]
-        core[p, d, e] = send(part, part, sc.at[p, d, e], rc.at[p, d, e], nav.peer("c", 1))
+        core[p, d, e] = send(part, part, sc.at[p], rc.at[p, d, e], nav.peer("c", 1))
+
+    def pass_on(p, e, d, source):
+        part = full.at[p, c, (place[p][2] + 4 - source) % 4, (place[p][1] + 4 - e) % 4]
+        slot = d if source == 0 else 2
+        third[p, e, slot] = send(part, part, s3.at[p], r3.at[p, e, slot - 1], nav.peer(ORDERS[p][2], d))
 
     def spread(p, e):
-        part = full.at[p, c, place[p][2], (place[p][1] + 4 - e) % 4]
-        for d in (2, 1, 3):
-            third[p, e, d] = send(part, part, s3.at[p, e, d - 1], r3.at[p, e, d - 1], nav.peer(ORDERS[p][2], d))
+        pass_on(p, e, 1, 0)
+        pass_on(p, e, 3, 0)
         share(p, 0, e)
 
-    def collect(d):
-        for e in (0, 1, 3, 2):
-            for p in range(3):
+    def collect(e):
+        for p in range(3):
+            for d in (1, 3):
                 third[p, e, d].wait_recv()
+                if (e % 2 == 0) == (d == 1):
+                    pass_on(p, e, d, d)
                 share(p, d, e)
 
-    def units(d):
+    def units(*ds):
         for p in range(3):
-            for e in range(4):
-                core[p, d, e].wait_recv()
-            unit(p, (place[p][2] + 4 - d) % 4)
+            for d in ds:
+                for e in range(4):
+                    core[p, d, e].wait_recv()
+            unit(p, [(place[p][2] + 4 - d) % 4 for d in ds])
 
     for p, order in enumerate(ORDERS):
         i1, i2, i3 = place[p]
         block = full.at[p, c, i3, i2, i1]
         for d in (2, 1, 3):
-            first[p, d] = send(block, block, s1.at[p, d - 1], r1.at[p, d - 1], nav.peer(order[0], d))
+            first[p, d] = send(block, block, s1.at[p], r1.at[p, d - 1], nav.peer(order[0], d))
     filler(0)
     for p, order in enumerate(ORDERS):
         i1, i2, i3 = place[p]
-        for d in (1, 2, 3):
+        for d in (1, 3, 2):
             first[p, d].wait_recv()
         part = full.at[p, c, i3, i2]
         for d in (2, 1, 3):
-            second[p, d] = send(part, part, s2.at[p, d - 1], r2.at[p, d - 1], nav.peer(order[1], d))
+            second[p, d] = send(part, part, s2.at[p], r2.at[p, d - 1], nav.peer(order[1], d))
+    for p in range(3):
         spread(p, 0)
     filler(1)
     for e in (1, 3, 2):
         for p in range(3):
             second[p, e].wait_recv()
             spread(p, e)
+    collect(0)
     filler(2)
     units(0)
-    collect(1)
-    collect(3)
-    units(1)
-    collect(2)
-    units(3)
+    for e in (1, 3, 2):
+        collect(e)
+    units(1, 3)
+    for e in (0, 1, 3, 2):
+        for p in range(3):
+            third[p, e, 2].wait_recv()
+            share(p, 2, e)
     units(2)
-    for group in (first, second, third, core):
-        for copy in group.values():
-            copy.wait_send()
+
+    def drain():
+        for p in range(3):
+            i1, i2, i3 = place[p]
+            drained(full.at[p, c, i3, i2, 0:3], s1.at[p], r1.at[p, 0], nav.peer("c", 1))
+            drained(full.at[p, c, i3, 0:3], s2.at[p], r1.at[p, 0], nav.peer("c", 1))
+            drained(full.at[p, c, 0:3], s3.at[p], r1.at[p, 0], nav.peer("c", 1))
+            drained(full.at[p, c], sc.at[p], r1.at[p, 0], nav.peer("c", 1))
+
+    return drain
 
 
 def columns(w, p):
@@ -143,6 +167,19 @@
     if p == 1:
         return ()
     return (slice(None), slice(None), k3)
+
+
+def slab_product(p, ks, full, weights, total):
+    if p == 1:
+        left = jnp.concatenate([flat(full[1, :, k]) for k in ks], axis=1)
+        total[...] = (flat(total[...]) + weights(ks, left)).reshape(total.shape)
+        return
+    take = (lambda k, w: flat(full[0, :, k, :, w])) if p == 0 else (lambda k, w: flat(full[2, :, k, w]))
+    left = jnp.concatenate([jnp.concatenate([take(k, w) for w in range(4)], axis=1) for k in ks], axis=0)
+    t = weights(range(4), left)
+    for j, k in enumerate(ks):
+        dst = slab_rows(p, k) + (Ellipsis,)
+        total[dst] = total[dst] + t[j * 128 : j * 128 + 128].reshape(2, 4, 16, 512)
 
 
 def slab_pieces(p, k3):
@@ -178,30 +215,31 @@
     return jnp.concatenate(rows, axis=1)
 
 
-def front(nav, doc_ref, gain_ref, post_ref, bias_row, loads, refs):
+def front(nav, doc_ref, gain_ref, post_ref, bias_row, loads, greeted, norm_piece, refs):
     (xv, cosv, sinv, wq, wk, wv, wo, part32, part16, got1, ss1, got_ss, s1, r1, s1b, r1b,
      kv, s3, r3, mixed, s5, r5, proj, got7, s7, r7, sq8, got8, s8, r8) = refs
     h, y, x = nav.h, nav.y, nav.x
     loads["x"].wait()
     xf = xv[...].astype(F32)
+    scaled = (xf * row_of(gain_ref)).astype(BF)
+    for name in ("q", "k", "v"):
+        loads[name].wait()
+    loads["dec"].start()
+    loads["enc"].start()
+    query = jnp.dot(scaled, wq[...], preferred_element_type=F32)
+    key = jnp.dot(scaled, wk[...], preferred_element_type=F32)
+    val = jnp.dot(scaled, wv[...], preferred_element_type=F32)
+    for w in range(4):
+        kvh = w // 2 * 128
+        for k, t in enumerate((query[:, w * 128 : w * 128 + 128], key[:, kvh : kvh + 128], val[:, kvh : kvh + 128])):
+            part32[w, :, k * 128 : k * 128 + 128] = t
+            part16[w, :, k * 128 : k * 128 + 128] = t.astype(BF)
+    greeted()
+    moved = [send(part16.at[(y + d) % 4], got1.at[d - 1], s1.at[d - 1], r1.at[d - 1], nav.peer("y", d)) for d in (2, 1, 3)]
     ss1[...] = lax.dot_general(
         jnp.ones((8, 1152), F32), xf * xf, (((1,), (1,)), ((), ())), precision=HIGHEST, preferred_element_type=F32
     )
     square = [send(ss1, got_ss.at[d - 1], s1b.at[d - 1], r1b.at[d - 1], nav.peer("y", d)) for d in (1, 2, 3)]
-    scaled = (xf * row_of(gain_ref)).astype(BF)
-    for name in ("q", "k", "v"):
-        loads[name].wait()
-    for kvh in range(2):
-        cols = slice(kvh * 128, kvh * 128 + 128)
-        key = jnp.dot(scaled, wk[:, cols], preferred_element_type=F32)
-        val = jnp.dot(scaled, wv[:, cols], preferred_element_type=F32)
-        for g in range(2):
-            w = kvh * 2 + g
-            q = jnp.dot(scaled, wq[:, w * 128 : w * 128 + 128], preferred_element_type=F32)
-            for k, t in enumerate((q, key, val)):
-                part32[w, :, k * 128 : k * 128 + 128] = t
-                part16[w, :, k * 128 : k * 128 + 128] = t.astype(BF)
-    moved = [send(part16.at[(y + d) % 4], got1.at[d - 1], s1.at[d - 1], r1.at[d - 1], nav.peer("y", d)) for d in (2, 1, 3)]
     bounds = []
     run = 0
     for j in range(4):
@@ -234,6 +272,8 @@
     kv[x, :, 0:128] = qkv[1]
     kv[x, :, 128:256] = qkv[2]
     spreads = [send(kv.at[x], kv.at[x], s3.at[d - 1], r3.at[d - 1], nav.peer("x", d)) for d in (2, 1, 3)]
+    loads["dec"].wait()
+    norm_piece(0)
     for copy in spreads:
         copy.wait_recv()
     keys = kv[:, :, 0:128].reshape(512, 128)
@@ -253,6 +293,7 @@
         t = jnp.dot(whole, wo[:, cols], preferred_element_type=F32).astype(BF)
         proj[:, :, cols] = t.reshape(8, 16, 384)
     parts = [send(proj.at[(h + d) % 8], got7.at[d - 1], s7.at[d - 1], r7.at[d - 1], nav.peer("h", d)) for d in range(1, 8)]
+    norm_piece(1)
     for copy in parts:
         copy.wait_recv()
     acc = proj[h].astype(F32)
@@ -261,6 +302,7 @@
     acc = acc.astype(BF).astype(F32)
     sq8[...] = jnp.broadcast_to(jnp.sum(acc * acc, axis=1, keepdims=True), (16, 128))
     norms = [send(sq8, got8.at[d - 1], s8.at[d - 1], r8.at[d - 1], nav.peer("y", d)) for d in (2, 1, 3)]
+    norm_piece(2)
     for copy in norms:
         copy.wait_recv()
     inverse_post = lax.rsqrt((sq8[...] + got8[0] + got8[1] + got8[2]) / D + norm_eps)[:, 0:1]
@@ -274,9 +316,9 @@
 def step_kernel(
     doc_ref, gain_ref, post_ref, bias_ref, ebias_ref, x_hbm, cos_hbm, sin_hbm, wq_hbm, wk_hbm, wv_hbm, wo_hbm,
     enc_hbm, dec_hbm,
-    cent_hbm, grad_hbm, acts_ref, gpre_ref, coef_ref, loss_ref,
-    enc, dec, lsem, osem, resid_ref, full, pre, norms, norm_row,
-    part, got0, s0, r0, got3, s3, r3, slab, got2, s2, r2, strip, got1, s1, r1,
+    cent_hbm, grad_hbm, flipped_ref, gpre_ref, coef_ref, loss_ref,
+    acts_ref, enc, dec, lsem, osem, resid_ref, full, pre, norms, norm_row,
+    part, got0, s0, r0, relay, got3, s3, r3, slab, got2, s2, r2, strip, got1, s1, r1,
     pool_h, pool_y, pool_x, sl, rl, gfull, *rest,
 ):
     fsems, gsems, frefs = rest[:8], rest[8:16], rest[16:]
@@ -292,48 +334,51 @@
         ("dec", dec_hbm, dec), ("enc", enc_hbm, enc),
     ]):
         loads[name] = pltpu.make_async_copy(src, dst, lsem.at[k])
-        loads[name].start()
-    barrier(nav)
+        if k < 7:
+            loads[name].start()
+    greeted = greet(nav)
+
+    def norm_piece(k):
+        if k == 2:
+            sums = lax.dot_general(
+                jnp.ones((8, 128), F32), norms[...], (((1,), (1,)), ((), ())), precision=HIGHEST, preferred_element_type=F32
+            )
+            norm_row[...] = jnp.sqrt(sums + norm_eps)
+            pre[...] = jnp.zeros(pre.shape, F32)
+            return
+
+        def body(j, carry):
+            r = pl.ds(pl.multiple_of(j * 32, 32), 32)
+            t = jnp.zeros((32, 128), F32)
+            for m in range(36):
+                v = dec[r, m * 128 : m * 128 + 128].astype(F32)
+                t = t + v * v
+            norms[r, :] = t
+            return carry
+
+        lax.fori_loop(k * 8, k * 8 + 8, body, 0)
+
     bias_row = row_of(bias_ref, y)
-    resid, centered, sends = front(nav, doc_ref, gain_ref, post_ref, bias_row, loads, frefs[:-1])
+    resid, centered, sends = front(nav, doc_ref, gain_ref, post_ref, bias_row, loads, greeted, norm_piece, frefs[:-1])
     resid_ref[...] = resid
     for p in range(3):
         i1, i2, i3 = place[p]
         full[p, c, i3, i2, i1] = centered[:, p * 384 : p * 384 + 384]
 
-    def norms_filler(k):
-        if k == 0:
-            loads["dec"].wait()
+    def before_encode(k):
+        if k == 2:
             loads["enc"].wait()
 
-            def body(j, carry):
-                r = pl.ds(pl.multiple_of(j * 32, 32), 32)
-                t = jnp.zeros((32, 128), F32)
-                for m in range(36):
-                    v = dec[r, m * 128 : m * 128 + 128].astype(F32)
-                    t = t + v * v
-                norms[r, :] = t
-                return carry
-
-            lax.fori_loop(0, 16, body, 0)
-            pre[...] = jnp.zeros(pre.shape, F32)
-        if k == 1:
-            sums = lax.dot_general(
-                jnp.ones((8, 128), F32), norms[...], (((1,), (1,)), ((), ())), precision=HIGHEST, preferred_element_type=F32
-            )
-            norm_row[...] = jnp.sqrt(sums + norm_eps)
-
-    def encode(p, k3):
-        dst = slab_rows(p, k3) + (Ellipsis,)
-        t = pre[dst]
-        shape = t.shape
-        t = flat(t)
-        for idx, w in slab_pieces(p, k3):
-            t = t + jnp.dot(flat(full[idx]), enc[columns(w, p), :], preferred_element_type=F32)
-        pre[dst] = t.reshape(shape)
-        unpack(full, cent_hbm, osem.at[0], p, k3)
-
-    all_gather(nav, full, fsems, norms_filler, encode)
+    def encode(p, ks):
+        def product(ws, left):
+            rows = jnp.concatenate([enc[columns(w, p), :] for w in ws], axis=0)
+            return jnp.dot(left, rows, preferred_element_type=F32)
+
+        slab_product(p, ks, full, product, pre)
+        for k in ks:
+            unpack(full, cent_hbm, osem.at[0], p, k)
+
+    drain_full = all_gather(nav, full, fsems, before_encode, encode)
     act_sum = jnp.zeros((1, 512), F32)
     ebias = row_of(ebias_ref)
     for k in range(2):
@@ -347,34 +392,87 @@
 
     swap, third, second, first = {}, {}, {}, {}
 
-    def produce(p, d):
+    def exchange(p, d):
         t3 = (place[p][2] + d) % 4
-        left = flat(acts_ref[slab_rows(p, t3) + (Ellipsis,)])
-        for idx, w in slab_pieces(p, t3):
-            t = jnp.dot(left, dec[:, columns(w, p)], preferred_element_type=F32).astype(BF)
-            part[idx] = t.reshape((2, 4, 4, 16, 384) if p == 1 else (2, 4, 16, 384))
         swap[p, d] = send(part.at[p, 1 - c, t3], got0.at[p, t3], s0.at[p, d], r0.at[p, d], nav.peer("c", 1))
 
-    def combine(p, d):
-        t3 = (place[p][2] + d) % 4
-        swap[p, d].wait_recv()
-        if d:
-            part[p, c, t3] = (part[p, c, t3].astype(F32) + got0[p, t3].astype(F32)).astype(BF)
-            third[p, d] = send(part.at[p, c, t3], got3.at[p, d - 1], s3.at[p, d - 1], r3.at[p, d - 1], nav.peer(ORDERS[p][2], d))
-
-    order = [(p, d) for d in (2, 1, 3, 0) for p in (1, 0, 2)]
-    for k, (p, d) in enumerate(order):
-        produce(p, d)
-        if k:
-            combine(*order[k - 1])
-    combine(*order[-1])
+    def produce(p, *ws):
+        cols = jnp.concatenate([dec[:, columns(w, p)] for w in ws], axis=1)
+        both = jnp.dot(flat(acts_ref[...]), cols, preferred_element_type=F32).astype(BF)
+        for j, w in enumerate(ws):
+            t = both[:, j * 384 : j * 384 + 384].reshape(2, 4, 4, 16, 384)
+            if p == 1:
+                part[1, :, w] = t
+            elif p == 0:
+                part[0, :, :, :, w] = t
+            else:
+                for z in range(4):
+                    part[2, :, :, w, z] = t[:, z]
+
+    def out3(p, slot, src, dst, d):
+        third[p, slot] = send(src, dst, s3.at[p, slot], r3.at[p, slot], nav.peer(ORDERS[p][2], d))
+
+    def chip_sum(p, t3, k):
+        return part[p, c, t3, k : k + 2].astype(F32) + got0[p, t3, k : k + 2].astype(F32)
+
+    def far(p):
+        t3 = (place[p][2] + 2) % 4
+        swap[p, 2].wait_recv()
+        for k, d in ((0, 1), (2, 3)):
+            half = part.at[p, c, t3, k : k + 2]
+            half[...] = chip_sum(p, t3, k).astype(BF)
+            out3(p, k // 2, half, relay.at[p, k // 2], d)
+
+    def near(p):
+        for d, k in ((1, 2), (3, 0)):
+            t3 = (place[p][2] + d) % 4
+            swap[p, d].wait_recv()
+            half = part.at[p, c, t3, k : k + 2]
+            half[...] = chip_sum(p, t3, k).astype(BF)
+            out3(p, d + 1, half, got3.at[p, d // 2, k : k + 2], d)
+
+    def joined(p):
+        for d, k in ((1, 0), (3, 2)):
+            t3 = (place[p][2] + d) % 4
+            third[p, d // 2].wait_recv()
+            half = part.at[p, c, t3, k : k + 2]
+            half[...] = (chip_sum(p, t3, k) + relay[p, d // 2].astype(F32)).astype(BF)
+            out3(p, d + 2, half, got3.at[p, d // 2, k : k + 2], d)
+
+    produce(1, (y + 2) % 4)
+    exchange(1, 2)
+    produce(1, (y + 1) % 4, (y + 3) % 4)
+    exchange(1, 1)
+    exchange(1, 3)
+    produce(0, 0, 1)
+    far(1)
+    produce(0, 2, 3)
+    for d in (2, 1, 3, 0):
+        exchange(0, d)
+    near(1)
+    produce(2, 0, 1)
+    far(0)
+    near(0)
+    produce(2, 2, 3)
+    for d in (2, 1, 3, 0):
+        exchange(2, d)
+    produce(1, y)
+    exchange(1, 0)
+    far(2)
+    near(2)
+    joined(1)
+    joined(0)
+    for k in range(2):
+        flipped_ref[:, k * 256 : k * 256 + 256] = flat(acts_ref[k]).T
+    joined(2)
+    for p in range(3):
+        swap[p, 0].wait_recv()
     for p in range(3):
         i1, i2, i3 = place[p]
-        for d in (1, 2, 3):
-            third[p, d].wait_recv()
+        for slot in (2, 3, 4, 5):
+            third[p, slot].wait_recv()
         t = part[p, c, i3].astype(F32) + got0[p, i3].astype(F32)
-        for d in range(3):
-            t = t + got3[p, d].astype(F32)
+        t = t + got3[p, 0].astype(F32) + got3[p, 1].astype(F32)
         slab[p] = t.astype(BF)
         for d in (2, 1, 3):
             second[p, d] = send(slab.at[p, (i2 + d) % 4], got2.at[p, d - 1], s2.at[p, d - 1], r2.at[p, d - 1], nav.peer(ORDERS[p][1], d))
@@ -432,24 +530,23 @@
     upstream = frefs[-1]
     upstream[...] = jnp.zeros(upstream.shape, F32)
 
-    def decode(p, k3):
-        dst = slab_rows(p, k3) + (Ellipsis,)
-        t = upstream[dst]
-        shape = t.shape
-        t = flat(t)
-        for idx, w in slab_pieces(p, k3):
-            t = t + lax.dot_general(
-                flat(gfull[idx]), dec[:, columns(w, p)], (((1,), (1,)), ((), ())), preferred_element_type=F32
-            )
-        upstream[dst] = t.reshape(shape)
-        unpack(gfull, grad_hbm, osem.at[1], p, k3)
-
-    all_gather(nav, gfull, gsems, loss_filler, decode)
+    def decode(p, ks):
+        def product(ws, left):
+            cols = jnp.concatenate([dec[:, columns(w, p)] for w in ws], axis=1)
+            return lax.dot_general(left, cols, (((1,), (1,)), ((), ())), preferred_element_type=F32)
+
+        slab_product(p, ks, gfull, product, upstream)
+        for k in ks:
+            unpack(gfull, grad_hbm, osem.at[1], p, k)
+
+    drain_gfull = all_gather(nav, gfull, gsems, loss_filler, decode)
     loss_ref[...] = pool_sum(2) / (TOKENS * D)
     lift = (l1_weight / TOKENS) * norm_row[0:1]
     for k in range(2):
         t = jnp.where(flat(pre[k]) > 0, flat(upstream[k]) + lift, 0.0).astype(BF)
         gpre_ref[k] = t.reshape(4, 4, 16, 512)
+    drain_full()
+    drain_gfull()
     for group in (swap, third, second, first):
         for copy in group.values():
             copy.wait_send()
@@ -479,16 +576,16 @@
         name="step",
         out_shape=(
             jax.ShapeDtypeStruct((2, 4, 4, 16, D), BF), jax.ShapeDtypeStruct((2, 4, 4, 16, D), BF),
-            jax.ShapeDtypeStruct((2, 4, 4, 16, 512), BF), jax.ShapeDtypeStruct((2, 4, 4, 16, 512), BF),
+            jax.ShapeDtypeStruct((512, 512), BF), jax.ShapeDtypeStruct((2, 4, 4, 16, 512), BF),
             jax.ShapeDtypeStruct((8, 512), F32), jax.ShapeDtypeStruct((8, 128), F32),
         ),
         in_specs=[pl.BlockSpec(memory_space=pltpu.SMEM)] + [vmem] * 4 + [anyspace] * 9,
         out_specs=(anyspace, anyspace, vmem, vmem, vmem, vmem),
         scratch_shapes=[
-            V((D, 512), BF), V((512, D), BF), dma((9,)), dma((2,)), V((16, 1152), BF),
+            V((2, 4, 4, 16, 512), BF), V((D, 512), BF), V((512, D), BF), dma((9,)), dma((2,)), V((16, 1152), BF),
             V((3, 2, 4, 4, 4, 16, 384), BF), V((2, 4, 4, 16, 512), F32), V((512, 128), F32), V((8, 512), F32),
             V((3, 2, 4, 4, 4, 16, 384), BF), V((3, 4, 4, 4, 16, 384), BF), dma((3, 4)), dma((3, 4)),
-            V((3, 3, 4, 4, 16, 384), BF), dma((3, 3)), dma((3, 3)),
+            V((3, 2, 2, 4, 16, 384), BF), V((3, 2, 4, 4, 16, 384), BF), dma((3, 6)), dma((3, 6)),
             V((3, 4, 4, 16, 384), BF), V((3, 3, 4, 16, 384), BF), dma((3, 3)), dma((3, 3)),
             V((3, 4, 16, 384), BF), V((3, 3, 16, 384), BF), dma((3, 3)), dma((3, 3)),
             V((8, 8, 128), F32), V((4, 8, 128), F32), V((4, 8, 128), F32), dma((3, 7)), dma((3, 7)),
@@ -496,6 +593,42 @@
         ] + gather_sems() + gather_sems() + front_scratch + [V((2, 4, 4, 16, 512), F32)],
         compiler_params=pltpu.CompilerParams(collective_id=0, has_side_effects=True, vmem_limit_bytes=60 << 20),
     )(*args)
+
+
+def grads_kernel(cent_ref, gpre_ref, grad_ref, flipped_ref, dec_ref, coef_ref, loss_in, genc_ref, gdec_ref, loss_out, lift):
+    @pl.when(pl.program_id(0) == 0)
+    def _():
+        lift[...] = lax.dot_general(
+            coef_ref[...], jnp.full((8, 128), 0.125, F32), (((0,), (0,)), ((), ())), precision=HIGHEST, preferred_element_type=F32
+        )
+        loss_out[0, 0] = loss_in[0, 0]
+
+    t = jnp.dot(flipped_ref[...], grad_ref[...], preferred_element_type=F32)
+    for m in range(t.shape[1] // 128):
+        cols = slice(m * 128, m * 128 + 128)
+        gdec_ref[:, cols] = (t[:, cols] + lift[...] * dec_ref[:, cols].astype(F32)).astype(BF)
+    genc_ref[...] = lax.dot_general(
+        cent_ref[...], gpre_ref[...], (((0,), (0,)), ((), ())), preferred_element_type=F32
+    ).astype(BF)
+
+
+def grads(centered, grad_pre, grad_recon, acts, dec, coef, loss):
+    tall = pl.BlockSpec((512, 768), lambda j: (0, j))
+    square = pl.BlockSpec((512, 512), lambda j: (0, 0))
+    return pl.pallas_call(
+        grads_kernel,
+        name="grads",
+        grid=(6,),
+        out_shape=(
+            jax.ShapeDtypeStruct((D, 512), BF), jax.ShapeDtypeStruct((512, D), BF), jax.ShapeDtypeStruct((1, 1), F32)
+        ),
+        in_specs=[
+            tall, square, tall, square, tall, pl.BlockSpec((8, 512), lambda j: (0, 0)), pl.BlockSpec(memory_space=pltpu.SMEM),
+        ],
+        out_specs=(pl.BlockSpec((768, 512), lambda j: (j, 0)), tall, pl.BlockSpec(memory_space=pltpu.SMEM)),
+        scratch_shapes=[pltpu.VMEM((512, 128), F32)],
+        compiler_params=pltpu.CompilerParams(dimension_semantics=("arbitrary",), vmem_limit_bytes=63 << 20),
+    )(centered, grad_pre, grad_recon, acts, dec, coef, loss)
 
 
 def rope_tables():
@@ -516,11 +649,9 @@
         w_query, w_key, w_value, w_out, enc_weight, dec_weight,
     )
     centered, grad_recon = centered.reshape(TOKENS, D), grad_recon.reshape(TOKENS, D)
-    acts, grad_pre = acts.reshape(TOKENS, 512), grad_pre.reshape(TOKENS, 512)
-    grad_enc = lax.dot_general(centered, grad_pre, (((0,), (0,)), ((), ())), preferred_element_type=F32).astype(BF)
-    decoder_term = lax.dot_general(acts, grad_recon, (((0,), (0,)), ((), ())), preferred_element_type=F32)
-    grad_dec = (decoder_term + coef[0][:, None] * dec_weight.astype(F32)).astype(BF)
-    return (grad_enc, grad_dec, loss[0, 0])
+    grad_pre = grad_pre.reshape(TOKENS, 512)
+    grad_enc, grad_dec, total = grads(centered, grad_pre, grad_recon, acts, dec_weight, coef, loss)
+    return (grad_enc, grad_dec, total.reshape(()))
 
 
 def solution(mesh):

time: 128 us -> 116 us (0.906)
  matrix products: 13.3 us -> 0 us
  Pallas kernels: 112 us -> 115 us
  local copies, waits for them, and re-layouts: 1.91 us -> 0 us
    dot_general x2 -> x0, matrix products: 13.3 us -> none  [the longest x1 9 us: per_device(): lax.dot_general(acts, grad_recon, (((0,), (0,)), ((), ())), preferred_ele...]
    pallas_call x0 -> x1, Pallas kernels: none -> 12.5 us  [grads(): pl.pallas_call(grads_kernel, name='grads', grid=(6,), out_shape=(jax.Shap...]
    pallas_call x1, Pallas kernels: 112 us -> 103 us  [step(): pl.pallas_call(step_kernel, name='step', out_shape=(jax.ShapeDtypeStruct(...]
    slice x2 -> x0, local copies, waits for them, and re-layouts: 1.9 us -> none  [the longest x1 1.18 us: per_device(): return (grad_enc, grad_dec, loss[0, 0])]
where the time goes in v3:
time: 116 us
  Pallas kernels  115 us (99%)
    pallas_call x1, Pallas kernels, step(): pl.pallas_call(step_kernel, name='step', out_shape=(jax.ShapeDtypeStruct(...  103 us
    pallas_call x1, Pallas kernels, grads(): pl.pallas_call(grads_kernel, name='grads', grid=(6,), out_shape=(jax.Shap...  12.5 us

profile of v3, /device:TPU:1, one launch (start us, length us, event | category | flops | bytes accessed | tf_op | source)
XLA Modules:
  0.0 115.7 jit_solution(6506032593507250231)
XLA Ops:
  0.6 102.5 %step.1 = (bf16[2,4,4,16,4608]{4,3,2,1,0:T(8,128)(2,1)}, bf16[2,4,4,16,4608]{4,3,2,1,0:T(8,128)(2,1)}, bf16[512,512]{1,0:T(8,128)(2,1)}, bf16[2,4,4,16,512]{4,3,...) custom-call(s32[4]{0:T(128)} %doc_ref.1, f32[9,128]{1,0:T(8,128)} %bitcast.13, f32[36,128]{1,0:T(8,128)} %bitcast.11, ...), custom_call_target="tpu_custom_call" | custom-call | tf_op jit(solution)/shard_map/step/pallas_call | solution.py:574
  103.2 12.5 %grads.1 = (bf16[4608,512]{1,0:T(8,128)(2,1)}, bf16[512,4608]{1,0:T(8,128)(2,1)}, f32[1,1]{1,0:T(1,128)}) custom-call(bf16[512,4608]{1,0:T(8,128)(2,1)} %bitcast.8, bf16[512,512]{1,0:T(8,128)(2,1)} %bitcast.10, bf16[512,4608]{1,0:T(8,128)(2,1)} %bitcast.9, bf16[512,512]{1,0:T(8,128)(2,1)} %get-tuple-element.15.flipped_ref, bf16[512,4608]{1,0:T(8,128)(2,1)} %dec_ref.1, ...), custom_call_target="tpu_custom_call" | custom-call | tf_op jit(solution)/shard_map/grads/pallas_call | solution.py:618

commit v4 on v3

--- a/solution.py
+++ b/solution.py
@@ -76,7 +76,7 @@
     return [dma((3,)), dma((3, 3)), dma((3,)), dma((3, 3)), dma((3,)), dma((3, 4, 3)), dma((3,)), dma((3, 4, 4))]
 
 
-def all_gather(nav, full, sems, filler, unit):
+def all_gather(nav, full, sems, filler, unit, whole_strips=False):
     s1, r1, s2, r2, s3, r3, sc, rc = sems
     c = nav.c
     first, second, third, core = {}, {}, {}, {}
@@ -104,23 +104,31 @@
                     pass_on(p, e, d, d)
                 share(p, d, e)
 
-    def units(*ds):
-        for p in range(3):
-            for d in ds:
-                for e in range(4):
-                    core[p, d, e].wait_recv()
-            unit(p, [(place[p][2] + 4 - d) % 4 for d in ds])
+    def units(p, *ds):
+        for d in ds:
+            for e in range(4):
+                core[p, d, e].wait_recv()
+        unit(p, [(place[p][2] + 4 - d) % 4 for d in ds])
+
+    def relayed(*es):
+        for e in es:
+            for p in range(3):
+                third[p, e, 2].wait_recv()
+                share(p, 2, e)
 
     for p, order in enumerate(ORDERS):
         i1, i2, i3 = place[p]
         block = full.at[p, c, i3, i2, i1]
         for d in (2, 1, 3):
+            if whole_strips:
+                continue
             first[p, d] = send(block, block, s1.at[p], r1.at[p, d - 1], nav.peer(order[0], d))
     filler(0)
     for p, order in enumerate(ORDERS):
         i1, i2, i3 = place[p]
         for d in (1, 3, 2):
-            first[p, d].wait_recv()
+            if not whole_strips:
+                first[p, d].wait_recv()
         part = full.at[p, c, i3, i2]
         for d in (2, 1, 3):
             second[p, d] = send(part, part, s2.at[p], r2.at[p, d - 1], nav.peer(order[1], d))
@@ -133,20 +141,24 @@
             spread(p, e)
     collect(0)
     filler(2)
-    units(0)
+    for p in range(3):
+        units(p, 0)
     for e in (1, 3, 2):
         collect(e)
-    units(1, 3)
-    for e in (0, 1, 3, 2):
-        for p in range(3):
-            third[p, e, 2].wait_recv()
-            share(p, 2, e)
-    units(2)
+    units(0, 1, 3)
+    relayed(0)
+    units(1, 1, 3)
+    relayed(1, 3)
+    units(2, 1, 3)
+    relayed(2)
+    for p in range(3):
+        units(p, 2)
 
     def drain():
         for p in range(3):
             i1, i2, i3 = place[p]
-            drained(full.at[p, c, i3, i2, 0:3], s1.at[p], r1.at[p, 0], nav.peer("c", 1))
+            if not whole_strips:
+                drained(full.at[p, c, i3, i2, 0:3], s1.at[p], r1.at[p, 0], nav.peer("c", 1))
             drained(full.at[p, c, i3, 0:3], s2.at[p], r1.at[p, 0], nav.peer("c", 1))
             drained(full.at[p, c, 0:3], s3.at[p], r1.at[p, 0], nav.peer("c", 1))
             drained(full.at[p, c], sc.at[p], r1.at[p, 0], nav.peer("c", 1))
@@ -271,11 +283,18 @@
         qkv.append(t.astype(BF))
     kv[x, :, 0:128] = qkv[1]
     kv[x, :, 128:256] = qkv[2]
-    spreads = [send(kv.at[x], kv.at[x], s3.at[d - 1], r3.at[d - 1], nav.peer("x", d)) for d in (2, 1, 3)]
+    later = []
+    for d in (2, 1, 3):
+        copy = pltpu.make_async_remote_copy(
+            src_ref=kv.at[x], dst_ref=kv.at[x], send_sem=s3.at[d - 1], recv_sem=r3.at[d - 1],
+            device_id=nav.peer("x", d), device_id_type=MESH,
+        )
+        pl.when(x + d < 4)(copy.start)
+        later.append((d, copy))
     loads["dec"].wait()
     norm_piece(0)
-    for copy in spreads:
-        copy.wait_recv()
+    for d, copy in later:
+        pl.when(x >= d)(copy.wait_recv)
     keys = kv[:, :, 0:128].reshape(512, 128)
     vals = kv[:, :, 128:256].reshape(512, 128)
     scores = lax.dot_general(qkv[0], keys, (((1,), (1,)), ((), ())), preferred_element_type=F32) * ((D // HEADS) ** -0.5)
@@ -309,16 +328,16 @@
     own_x = xv[pl.ds(pl.multiple_of(h * 16, 16), 16), :].astype(F32)
     resid = (own_x + acc * inverse_post * row_of(post_ref, y)).astype(BF)
     centered = (resid.astype(F32) - bias_row).astype(BF)
-    sends = square + moved + spreads + mixes + parts + norms
-    return resid, centered, sends
+    sends = square + moved + mixes + parts + norms
+    return resid, centered, sends, later
 
 
 def step_kernel(
     doc_ref, gain_ref, post_ref, bias_ref, ebias_ref, x_hbm, cos_hbm, sin_hbm, wq_hbm, wk_hbm, wv_hbm, wo_hbm,
     enc_hbm, dec_hbm,
     cent_hbm, grad_hbm, flipped_ref, gpre_ref, coef_ref, loss_ref,
-    acts_ref, enc, dec, lsem, osem, resid_ref, full, pre, norms, norm_row,
-    part, got0, s0, r0, relay, got3, s3, r3, slab, got2, s2, r2, strip, got1, s1, r1,
+    acts_ref, enc, dec, lsem, osem, strips, ss, rs, errors, full, pre, norms, norm_row,
+    part, got0, s0, r0, relay, got3, s3, r3, slab, got2, s2, r2, got1, s1, r1,
     pool_h, pool_y, pool_x, sl, rl, gfull, *rest,
 ):
     fsems, gsems, frefs = rest[:8], rest[8:16], rest[16:]
@@ -336,6 +355,8 @@
         loads[name] = pltpu.make_async_copy(src, dst, lsem.at[k])
         if k < 7:
             loads[name].start()
+    kv = frefs[16]
+    kv[...] = jnp.zeros(kv.shape, BF)
     greeted = greet(nav)
 
     def norm_piece(k):
@@ -359,11 +380,11 @@
         lax.fori_loop(k * 8, k * 8 + 8, body, 0)
 
     bias_row = row_of(bias_ref, y)
-    resid, centered, sends = front(nav, doc_ref, gain_ref, post_ref, bias_row, loads, greeted, norm_piece, frefs[:-1])
-    resid_ref[...] = resid
+    resid, centered, sends, later = front(nav, doc_ref, gain_ref, post_ref, bias_row, loads, greeted, norm_piece, frefs[:-1])
     for p in range(3):
         i1, i2, i3 = place[p]
         full[p, c, i3, i2, i1] = centered[:, p * 384 : p * 384 + 384]
+        strips[p, i1] = resid[:, p * 384 : p * 384 + 384]
 
     def before_encode(k):
         if k == 2:
@@ -379,6 +400,11 @@
             unpack(full, cent_hbm, osem.at[0], p, k)
 
     drain_full = all_gather(nav, full, fsems, before_encode, encode)
+    known = {}
+    for p, order in enumerate(ORDERS):
+        mine = strips.at[p, place[p][0]]
+        for d in (2, 1, 3):
+            known[p, d] = send(mine, mine, ss.at[p, d - 1], rs.at[p, d - 1], nav.peer(order[0], d))
     act_sum = jnp.zeros((1, 512), F32)
     ebias = row_of(ebias_ref)
     for k in range(2):
@@ -401,13 +427,7 @@
         both = jnp.dot(flat(acts_ref[...]), cols, preferred_element_type=F32).astype(BF)
         for j, w in enumerate(ws):
             t = both[:, j * 384 : j * 384 + 384].reshape(2, 4, 4, 16, 384)
-            if p == 1:
-                part[1, :, w] = t
-            elif p == 0:
-                part[0, :, :, :, w] = t
-            else:
-                for z in range(4):
-                    part[2, :, :, w, z] = t[:, z]
+            part[1, :, w] = t
 
     def out3(p, slot, src, dst, d):
         third[p, slot] = send(src, dst, s3.at[p, slot], r3.at[p, slot], nav.peer(ORDERS[p][2], d))
@@ -439,28 +459,45 @@
             half[...] = (chip_sum(p, t3, k) + relay[p, d // 2].astype(F32)).astype(BF)
             out3(p, d + 2, half, got3.at[p, d // 2, k : k + 2], d)
 
+    def produce_rows(p, ds, ws):
+        ts = [(place[p][2] + d) % 4 for d in ds]
+        left = jnp.concatenate([flat(acts_ref[slab_rows(p, t) + (Ellipsis,)]) for t in ts], axis=0)
+        cols = jnp.concatenate([dec[:, columns(w, p)] for w in ws], axis=1)
+        both = jnp.dot(left, cols, preferred_element_type=F32).astype(BF)
+        for j, t3 in enumerate(ts):
+            for i, w in enumerate(ws):
+                t = both[j * 128 : j * 128 + 128, i * 384 : i * 384 + 384].reshape(2, 4, 16, 384)
+                if p == 0:
+                    part[0, :, t3, :, w] = t
+                else:
+                    part[2, :, t3, w] = t
+
     produce(1, (y + 2) % 4)
     exchange(1, 2)
+    produce_rows(0, (2,), range(4))
+    exchange(0, 2)
+    produce_rows(2, (2,), range(4))
+    exchange(2, 2)
+    far(1)
     produce(1, (y + 1) % 4, (y + 3) % 4)
     exchange(1, 1)
     exchange(1, 3)
-    produce(0, 0, 1)
-    far(1)
-    produce(0, 2, 3)
-    for d in (2, 1, 3, 0):
+    far(0)
+    far(2)
+    produce_rows(0, (1, 3, 0), (0, 1))
+    near(1)
+    produce_rows(0, (1, 3, 0), (2, 3))
+    for d in (1, 3, 0):
         exchange(0, d)
-    near(1)
-    produce(2, 0, 1)
-    far(0)
+    produce_rows(2, (1, 3, 0), (0, 1))
     near(0)
-    produce(2, 2, 3)
-    for d in (2, 1, 3, 0):
+    produce_rows(2, (1, 3, 0), (2, 3))
+    for d in (1, 3, 0):
         exchange(2, d)
+    joined(1)
     produce(1, y)
     exchange(1, 0)
-    far(2)
     near(2)
-    joined(1)
     joined(0)
     for k in range(2):
         flipped_ref[:, k * 256 : k * 256 + 256] = flat(acts_ref[k]).T
@@ -483,21 +520,29 @@
         t = slab[p, i2].astype(F32)
         for d in range(3):
             t = t + got2[p, d].astype(F32)
-        strip[p] = t.astype(BF)
+        mine = got1.at[p, i1]
+        mine[...] = t.astype(BF)
         for d in (2, 1, 3):
-            first[p, d] = send(strip.at[p, (i1 + d) % 4], got1.at[p, d - 1], s1.at[p, d - 1], r1.at[p, d - 1], nav.peer(ORDERS[p][0], d))
+            first[p, d] = send(mine, mine, s1.at[p, d - 1], r1.at[p, d - 1], nav.peer(ORDERS[p][0], d))
     squares = jnp.zeros((16, 384), F32)
     for p in range(3):
         i1, i2, i3 = place[p]
-        cols = slice(p * 384, p * 384 + 384)
         for d in (1, 2, 3):
             first[p, d].wait_recv()
-        t = strip[p, i1].astype(F32)
-        for d in range(3):
-            t = t + got1[p, d].astype(F32)
-        error = t + bias_row[:, cols] - resid_ref[:, cols].astype(F32)
-        squares = squares + error * error
-        gfull[p, c, i3, i2, i1] = (2.0 / TOKENS * error).astype(BF)
+            known[p, d].wait_recv()
+        for j in range(4):
+            t = got1[p, 0, j].astype(F32)
+            for k in range(1, 4):
+                t = t + got1[p, k, j].astype(F32)
+            if p == 0:
+                bias = jnp.concatenate([bias_ref[j * 9 + k : j * 9 + k + 1] for k in range(3)], axis=1)
+            else:
+                bias = bias_row[:, p * 384 : p * 384 + 384]
+            error = t + bias - strips[p, j].astype(F32)
+            errors[j] = error
+            gfull[p, c, i3, i2, j] = (2.0 / TOKENS * error).astype(BF)
+        own = errors[i1]
+        squares = squares + own * own
 
     pools = [(pool_h, "h", 8, h), (pool_y, "y", 4, y), (pool_x, "x", 4, x)]
     losses = []
@@ -539,7 +584,7 @@
         for k in ks:
             unpack(gfull, grad_hbm, osem.at[1], p, k)
 
-    drain_gfull = all_gather(nav, gfull, gsems, loss_filler, decode)
+    drain_gfull = all_gather(nav, gfull, gsems, loss_filler, decode, whole_strips=True)
     loss_ref[...] = pool_sum(2) / (TOKENS * D)
     lift = (l1_weight / TOKENS) * norm_row[0:1]
     for k in range(2):
@@ -547,11 +592,13 @@
         gpre_ref[k] = t.reshape(4, 4, 16, 512)
     drain_full()
     drain_gfull()
-    for group in (swap, third, second, first):
+    for group in (swap, third, second, first, known):
         for copy in group.values():
             copy.wait_send()
     for copy in losses + sends:
         copy.wait_send()
+    for d, copy in later:
+        pl.when(x + d < 4)(copy.wait_send)
     pltpu.make_async_copy(cent_hbm, cent_hbm, osem.at[0]).wait()
     pltpu.make_async_copy(grad_hbm, grad_hbm, osem.at[1]).wait()
 
@@ -582,12 +629,12 @@
         in_specs=[pl.BlockSpec(memory_space=pltpu.SMEM)] + [vmem] * 4 + [anyspace] * 9,
         out_specs=(anyspace, anyspace, vmem, vmem, vmem, vmem),
         scratch_shapes=[
-            V((2, 4, 4, 16, 512), BF), V((D, 512), BF), V((512, D), BF), dma((9,)), dma((2,)), V((16, 1152), BF),
+            V((2, 4, 4, 16, 512), BF), V((D, 512), BF), V((512, D), BF), dma((9,)), dma((2,)), V((3, 4, 16, 384), BF), dma((3, 3)), dma((3, 3)), V((4, 16, 384), F32),
             V((3, 2, 4, 4, 4, 16, 384), BF), V((2, 4, 4, 16, 512), F32), V((512, 128), F32), V((8, 512), F32),
             V((3, 2, 4, 4, 4, 16, 384), BF), V((3, 4, 4, 4, 16, 384), BF), dma((3, 4)), dma((3, 4)),
             V((3, 2, 2, 4, 16, 384), BF), V((3, 2, 4, 4, 16, 384), BF), dma((3, 6)), dma((3, 6)),
             V((3, 4, 4, 16, 384), BF), V((3, 3, 4, 16, 384), BF), dma((3, 3)), dma((3, 3)),
-            V((3, 4, 16, 384), BF), V((3, 3, 16, 384), BF), dma((3, 3)), dma((3, 3)),
+            V((3, 4, 4, 16, 384), BF), dma((3, 3)), dma((3, 3)),
             V((8, 8, 128), F32), V((4, 8, 128), F32), V((4, 8, 128), F32), dma((3, 7)), dma((3, 7)),
             V((3, 2, 4, 4, 4, 16, 384), BF),
         ] + gather_sems() + gather_sems() + front_scratch + [V((2, 4, 4, 16, 512), F32)],

time: 116 us -> 113 us (0.974)
  Pallas kernels: 115 us -> 112 us
    pallas_call x1, Pallas kernels: 103 us -> 99.6 us  [step(): pl.pallas_call(step_kernel, name='step', out_shape=(jax.ShapeDtypeStruct(...]
where the time goes in v4:
time: 113 us
  Pallas kernels  112 us (99%)
    pallas_call x1, Pallas kernels, step(): pl.pallas_call(step_kernel, name='step', out_shape=(jax.ShapeDtypeStruct(...  99.6 us
    pallas_call x1, Pallas kernels, grads(): pl.pallas_call(grads_kernel, name='grads', grid=(6,), out_shape=(jax.Shap...  12.5 us

profile of v4, /device:TPU:1, one launch (start us, length us, event | category | flops | bytes accessed | tf_op | source)
XLA Modules:
  0.0 112.8 jit_solution(16524941560521352263)
XLA Ops:
  0.6 99.6 %step.1 = (bf16[2,4,4,16,4608]{4,3,2,1,0:T(8,128)(2,1)}, bf16[2,4,4,16,4608]{4,3,2,1,0:T(8,128)(2,1)}, bf16[512,512]{1,0:T(8,128)(2,1)}, bf16[2,4,4,16,512]{4,3,...) custom-call(s32[4]{0:T(128)} %doc_ref.1, f32[9,128]{1,0:T(8,128)} %bitcast.13, f32[36,128]{1,0:T(8,128)} %bitcast.11, ...), custom_call_target="tpu_custom_call" | custom-call | tf_op jit(solution)/shard_map/step/pallas_call | solution.py:621
  100.3 12.5 %grads.1 = (bf16[4608,512]{1,0:T(8,128)(2,1)}, bf16[512,4608]{1,0:T(8,128)(2,1)}, f32[1,1]{1,0:T(1,128)}) custom-call(bf16[512,4608]{1,0:T(8,128)(2,1)} %bitcast.8, bf16[512,512]{1,0:T(8,128)(2,1)} %bitcast.10, bf16[512,4608]{1,0:T(8,128)(2,1)} %bitcast.9, bf16[512,512]{1,0:T(8,128)(2,1)} %get-tuple-element.15.flipped_ref, bf16[512,4608]{1,0:T(8,128)(2,1)} %dec_ref.1, ...), custom_call_target="tpu_custom_call" | custom-call | tf_op jit(solution)/shard_map/grads/pallas_call | solution.py:665

commit v5 on v4

--- a/solution.py
+++ b/solution.py
@@ -234,6 +234,9 @@
     loads["x"].wait()
     xf = xv[...].astype(F32)
     scaled = (xf * row_of(gain_ref)).astype(BF)
+    ss1[...] = lax.dot_general(
+        jnp.ones((8, 1152), F32), xf * xf, (((1,), (1,)), ((), ())), precision=HIGHEST, preferred_element_type=F32
+    )
     for name in ("q", "k", "v"):
         loads[name].wait()
     loads["dec"].start()
@@ -247,11 +250,13 @@
             part32[w, :, k * 128 : k * 128 + 128] = t
             part16[w, :, k * 128 : k * 128 + 128] = t.astype(BF)
     greeted()
-    moved = [send(part16.at[(y + d) % 4], got1.at[d - 1], s1.at[d - 1], r1.at[d - 1], nav.peer("y", d)) for d in (2, 1, 3)]
-    ss1[...] = lax.dot_general(
-        jnp.ones((8, 1152), F32), xf * xf, (((1,), (1,)), ((), ())), precision=HIGHEST, preferred_element_type=F32
-    )
     square = [send(ss1, got_ss.at[d - 1], s1b.at[d - 1], r1b.at[d - 1], nav.peer("y", d)) for d in (1, 2, 3)]
+    moved = {}
+    for j, cols in enumerate((slice(128, 384), slice(0, 128))):
+        for d in (2, 1, 3):
+            moved[j, d] = send(
+                part16.at[(y + d) % 4, :, cols], got1.at[d - 1, :, cols], s1.at[d - 1, j], r1.at[d - 1, j], nav.peer("y", d)
+            )
     bounds = []
     run = 0
     for j in range(4):
@@ -271,18 +276,19 @@
     inverse = lax.rsqrt(spread / D + norm_eps)
     loads["cos"].wait()
     loads["sin"].wait()
-    for copy in moved:
-        copy.wait_recv()
-    qkv = []
-    for k in range(3):
+
+    def whole_sum(k):
         cols = slice(k * 128, k * 128 + 128)
         t = part32[y, :, cols] + got1[0, :, cols].astype(F32) + got1[1, :, cols].astype(F32) + got1[2, :, cols].astype(F32)
         t = t * inverse
         if k < 2:
             t = t * cosv[...] + pltpu.roll(t, 64, 1) * sinv[...]
-        qkv.append(t.astype(BF))
-    kv[x, :, 0:128] = qkv[1]
-    kv[x, :, 128:256] = qkv[2]
+        return t.astype(BF)
+
+    for d in (1, 2, 3):
+        moved[0, d].wait_recv()
+    kv[x, :, 0:128] = whole_sum(1)
+    kv[x, :, 128:256] = whole_sum(2)
     later = []
     for d in (2, 1, 3):
         copy = pltpu.make_async_remote_copy(
@@ -291,13 +297,16 @@
         )
         pl.when(x + d < 4)(copy.start)
         later.append((d, copy))
+    for d in (1, 2, 3):
+        moved[1, d].wait_recv()
+    own_query = whole_sum(0)
     loads["dec"].wait()
     norm_piece(0)
     for d, copy in later:
         pl.when(x >= d)(copy.wait_recv)
     keys = kv[:, :, 0:128].reshape(512, 128)
     vals = kv[:, :, 128:256].reshape(512, 128)
-    scores = lax.dot_general(qkv[0], keys, (((1,), (1,)), ((), ())), preferred_element_type=F32) * ((D // HEADS) ** -0.5)
+    scores = lax.dot_general(own_query, keys, (((1,), (1,)), ((), ())), preferred_element_type=F32) * ((D // HEADS) ** -0.5)
     capped = soft_cap * jnp.tanh(scores / soft_cap)
     weights = jnp.where(allowed, jnp.exp(capped), 0.0)
     probs = (weights / jnp.sum(weights, axis=-1, keepdims=True)).astype(BF)
@@ -328,7 +337,7 @@
     own_x = xv[pl.ds(pl.multiple_of(h * 16, 16), 16), :].astype(F32)
     resid = (own_x + acc * inverse_post * row_of(post_ref, y)).astype(BF)
     centered = (resid.astype(F32) - bias_row).astype(BF)
-    sends = square + moved + mixes + parts + norms
+    sends = square + list(moved.values()) + mixes + parts + norms
     return resid, centered, sends, later
 
 
@@ -612,7 +621,7 @@
         V((128, 1152), BF), V((128, 128), F32), V((128, 128), F32),
         V((1152, 512), BF), V((1152, 256), BF), V((1152, 256), BF), V((512, 1152), BF),
         V((4, 128, 384), F32), V((4, 128, 384), BF), V((3, 128, 384), BF),
-        V((8, 128), F32), V((3, 8, 128), F32), dma((3,)), dma((3,)), dma((3,)), dma((3,)),
+        V((8, 128), F32), V((3, 8, 128), F32), dma((3, 2)), dma((3, 2)), dma((3,)), dma((3,)),
         V((4, 128, 256), BF), dma((3,)), dma((3,)),
         V((4, 128, 128), BF), dma((3,)), dma((3,)),
         V((8, 16, 1152), BF), V((7, 16, 1152), BF), dma((7,)), dma((7,)),

time: 113 us -> 110 us (0.973)
  Pallas kernels: 112 us -> 109 us
    pallas_call x1, Pallas kernels: 99.6 us -> 96.7 us  [step(): pl.pallas_call(step_kernel, name='step', out_shape=(jax.ShapeDtypeStruct(...]
where the time goes in v5:
time: 110 us
  Pallas kernels  109 us (99%)
    pallas_call x1, Pallas kernels, step(): pl.pallas_call(step_kernel, name='step', out_shape=(jax.ShapeDtypeStruct(...  96.7 us
    pallas_call x1, Pallas kernels, grads(): pl.pallas_call(grads_kernel, name='grads', grid=(6,), out_shape=(jax.Shap...  12.5 us

profile of v5, /device:TPU:1, one launch (start us, length us, event | category | flops | bytes accessed | tf_op | source)
XLA Modules:
  0.0 109.9 jit_solution(3503621560060914965)
XLA Ops:
  0.6 96.7 %step.1 = (bf16[2,4,4,16,4608]{4,3,2,1,0:T(8,128)(2,1)}, bf16[2,4,4,16,4608]{4,3,2,1,0:T(8,128)(2,1)}, bf16[512,512]{1,0:T(8,128)(2,1)}, bf16[2,4,4,16,512]{4,3,...) custom-call(s32[4]{0:T(128)} %doc_ref.1, f32[9,128]{1,0:T(8,128)} %bitcast.13, f32[36,128]{1,0:T(8,128)} %bitcast.11, ...), custom_call_target="tpu_custom_call" | custom-call | tf_op jit(solution)/shard_map/step/pallas_call | solution.py:630
  97.4 12.5 %grads.1 = (bf16[4608,512]{1,0:T(8,128)(2,1)}, bf16[512,4608]{1,0:T(8,128)(2,1)}, f32[1,1]{1,0:T(1,128)}) custom-call(bf16[512,4608]{1,0:T(8,128)(2,1)} %bitcast.8, bf16[512,512]{1,0:T(8,128)(2,1)} %bitcast.10, bf16[512,4608]{1,0:T(8,128)(2,1)} %bitcast.9, bf16[512,512]{1,0:T(8,128)(2,1)} %get-tuple-element.15.flipped_ref, bf16[512,4608]{1,0:T(8,128)(2,1)} %dec_ref.1, ...), custom_call_target="tpu_custom_call" | custom-call | tf_op jit(solution)/shard_map/grads/pallas_call | solution.py:674
